TPU v7x, 128 devices: a whole 4x4x4 slice. The times are simulated.
128 devices in a mesh: shot: 4 (over y_hi, core), slab: 32 (over z, x, y_lo).
Axes of the slice: x: 4, y: 4 (y_hi: 2, y_lo: 2; y = y_hi * 2 + y_lo), z: 4, core: 2. Of those that a mesh axis runs over, the one named last changes fastest.
Arguments:
- source_field: bfloat16 [12, 8, 128, 256, 128], P('shot', None, 'slab'), may hold values from -4 to 4
- receiver_field: bfloat16 [12, 8, 128, 256, 128], P('shot', None, 'slab'), may hold values from -4 to 4
- shot_group: int32 [12], replicated, may hold values from 0 to 11
- first_weight: bfloat16 [32, 12, 3, 3, 3], replicated, may hold values from -0.3125 to 0.3125
- first_bias: float32 [32], replicated, may hold values from -3 to 3
- second_weight: bfloat16 [32, 32, 3, 3, 3], replicated, may hold values from -0.21875 to 0.21875
- second_bias: float32 [32], replicated, may hold values from -3 to 3
Outputs:
- features: bfloat16 [32, 128, 256, 128], P(None, 'shot', 'slab')
All inputs are finite; a program needn't handle non-finite values.
Results may differ from a plain program's by a relative error of at most 0.01.
Values may be sent and summed in bfloat16 or wider, within the bound.
No kernel may reach another device: no remote copies, remote signals or barrier semaphores. Data moves between devices by JAX's collectives and lax.ppermute only.
A program may use at most 128 MiB of HBM per device.

v0:
```python
import functools

import jax
import jax.numpy as jnp
from jax import lax
from jax.experimental import pallas as pl
from jax.experimental.pallas import tpu as pltpu
from jax.sharding import PartitionSpec as P

SC = 16

def cross_kernel(src_ref, rec_ref, out_ref, wide_ref):
    planes, nx, ny = src_ref.shape[2:]
    first = (pl.program_id(0) == 0) & (pl.program_id(1) == 0)
    edge = 2 * planes
    @pl.when(first)
    def _():
        wide_ref[0:edge, :] = jnp.zeros((edge, ny), jnp.float32)
        wide_ref[edge + planes * nx :, :] = jnp.zeros((edge, ny), jnp.float32)
    for z in range(planes):
        total = jnp.zeros((nx, ny), jnp.float32)
        for t in range(src_ref.shape[1]):
            total = total + src_ref[0, t, z].astype(jnp.float32) * rec_ref[0, t, z].astype(jnp.float32)
        wide_ref[pl.ds(edge + z, nx, stride=planes), :] = total
    rows = out_ref.shape[3]
    step = rows - 2 * edge
    for d in range(out_ref.shape[0]):
        out_ref[d, 0, 0] = wide_ref[d * step : d * step + rows, :].astype(out_ref.dtype)

def cross_pieces(source, receiver, targets):
    shots, steps, planes, nx, ny = source.shape
    halves = 2
    p = planes // halves
    rows = (nx // targets + 4) * p
    spec = pl.BlockSpec((1, steps, p, nx, ny), lambda s, h: (s, 0, h, 0, 0))
    return pl.pallas_call(
        cross_kernel,
        grid=(shots, halves),
        in_specs=[spec, spec],
        out_specs=pl.BlockSpec((targets, 1, 1, rows, ny), lambda s, h: (0, h, s, 0, 0)),
        out_shape=jax.ShapeDtypeStruct((targets, halves, shots, rows, ny), jnp.bfloat16),
        scratch_shapes=[pltpu.VMEM(((nx + 4) * p, ny), jnp.float32)],
        compiler_params=pltpu.CompilerParams(vmem_limit_bytes=48 << 20),
        name="cross",
    )(source, receiver)

def spread(part, bias):
    co = bias.shape[0]
    ny = part.shape[1]
    lane = lax.broadcasted_iota(jnp.int32, (co, ny), 1)
    low = jnp.where(lane == 0, 0.0, pltpu.roll(part[:co], 1, 1))
    high = jnp.where(lane == ny - 1, 0.0, pltpu.roll(part[2 * co :], ny - 1, 1))
    return jnp.maximum(part[co : 2 * co] + low + high + bias, 0.0)

def conv_kernel(place, group_ref, p0, p1, p2, p3, w1_ref, b1_ref, w2_ref, b2_ref,
                out_ref, x_ref, h_ref, gather_ref, k1_ref, k2_ref, bias_ref, turn_ref):
    co, ci = w1_ref.shape[1:]
    ny = x_ref.shape[-1]
    nhx = h_ref.shape[1]
    nox = out_ref.shape[2]
    nh = p0.shape[0]
    rows = p0.shape[2]
    shots = p0.shape[1]
    per = 2
    step = pl.program_id(0)
    zs = out_ref.shape[1]
    i, ni, j, nj = place()

    def hidden_row(z, live=None):
        for x in range(0, nhx, 2):
            right = jnp.concatenate(
                [jnp.concatenate([x_ref[z + dz, x + q + dx] for dz in range(3) for dx in range(3)], axis=0) for q in range(2)], axis=1)
            part = jnp.dot(k1_ref[...], right, preferred_element_type=jnp.float32)
            for q in range(2):
                v = spread(part[:, q * ny : (q + 1) * ny], bias_ref[0])
                if x + q == 0:
                    v = jnp.where(j > 0, v, 0.0)
                if x + q == nhx - 1:
                    v = jnp.where(j < nj - 1, v, 0.0)
                if live is not None:
                    v = jnp.where(live, v, 0.0)
                h_ref[z, x + q] = v.astype(h_ref.dtype)

    @pl.when(step == 0)
    def _():
        taps = 9
        w = k1_ref.shape[1]
        r = lax.broadcasted_iota(jnp.int32, (ci, w), 0)
        c = lax.broadcasted_iota(jnp.int32, (ci, w), 1)
        label = jnp.full((ci, w), -1, jnp.int32)
        for k in range(4):
            for s in range(shots):
                label = jnp.where(c % SC == k * shots + s, group_ref[(i ^ k) * shots + s], label)
        hit = r == label
        acc = jnp.zeros((3 * co, w), jnp.float32)
        for t in range(taps):
            pick = jnp.where(hit & (c // SC == t), 1.0, 0.0).astype(jnp.bfloat16)
            left = jnp.concatenate([w1_ref[3 * t + dy] for dy in range(3)], axis=0)
            acc = acc + jnp.dot(left, pick, preferred_element_type=jnp.float32)
            for dy in range(3):
                k2_ref[dy * co : (dy + 1) * co, t * co : (t + 1) * co] = w2_ref[3 * t + dy]
        k1_ref[...] = acc.astype(jnp.bfloat16)
        eye = lax.broadcasted_iota(jnp.int32, (co, co), 0) == lax.broadcasted_iota(jnp.int32, (co, co), 1)
        for n, b in enumerate((b1_ref, b2_ref)):
            col = jnp.sum(jnp.where(eye, jnp.broadcast_to(b[...], (co, co)), 0.0), axis=1, keepdims=True)
            bias_ref[n] = jnp.broadcast_to(col, (co, ny))
        gather_ref[...] = jnp.zeros(gather_ref.shape, jnp.float32)

        @pl.loop(0, nh)
        def _(l):
            want = l + jnp.where(i == 0, -1, jnp.where(i == ni - 1, 1, 0))
            here = jnp.clip(want, 0, nh - 1)
            keep = jnp.where(want == here, 1.0, 0.0)
            for k, p in enumerate((p0, p1, p2, p3)):
                for s in range(shots):
                    gather_ref[pl.ds(k * shots + s, rows, stride=SC), :] = p[here, s].astype(jnp.float32) * keep
            for x in range(rows // per):
                for z in range(per):
                    at = (x * per + z) * SC
                    x_ref[l * per + z, x] = gather_ref[at : at + SC, :].astype(jnp.bfloat16)

        for z in range(3):
            hidden_row(z)

        @pl.when(i == 0)
        def _():
            h_ref[0] = jnp.zeros(h_ref.shape[1:], h_ref.dtype)

    @pl.when(step == pl.num_programs(0))
    def _():
        out_ref[0, 0] = h_ref[step, 0, 0:8, :].astype(out_ref.dtype)
    @pl.loop(0, zs)
    def _(k):
        z = step * zs + k
        for x in range(0, nox, 2):
            right = jnp.concatenate(
                [jnp.concatenate([h_ref[z + dz, x + q + dx] for dz in range(3) for dx in range(3)], axis=0) for q in range(2)], axis=1)
            part = jnp.dot(k2_ref[...], right, preferred_element_type=jnp.float32)
            for q in range(2):
                turn_ref[pl.ds(x + q, co, stride=nox), :] = spread(part[:, q * ny : (q + 1) * ny], bias_ref[1])
        out_ref[:, k] = turn_ref[...].reshape(co, nox, ny).astype(out_ref.dtype)
        hidden_row(z + 3, (z != h_ref.shape[0] - 5) | (i < ni - 1))

def convolutions(place, shot_group, pieces, w1, b1, w2, b2, zs=4):
    nh, shots, rows, ny = pieces[0].shape
    nz = nh * 2 - 4
    nx = rows // 2 - 4
    co = w1.shape[0]
    ci = w1.shape[1]
    w1t = w1.transpose(2, 3, 4, 0, 1).reshape(27, co, ci)
    w2t = w2.transpose(2, 3, 4, 0, 1).reshape(27, co, co)
    whole = lambda a: pl.BlockSpec(a.shape, lambda s: (0,) * a.ndim)
    b1 = b1.reshape(1, co); b2 = b2.reshape(1, co)
    vm = [*pieces, w1t, b1, w2t, b2]
    return pl.pallas_call(
        functools.partial(conv_kernel, place),
        grid=(nz // zs,),
        in_specs=[pl.BlockSpec(memory_space=pltpu.SMEM)] + [whole(a) for a in vm],
        out_specs=pl.BlockSpec((co, zs, nx, ny), lambda s: (0, s, 0, 0)),
        out_shape=jax.ShapeDtypeStruct((co, nz, nx, ny), jnp.bfloat16),
        scratch_shapes=[
            pltpu.VMEM((nz + 5, nx + 4, SC, ny), jnp.bfloat16),
            pltpu.VMEM((nz + 3, nx + 2, co, ny), jnp.bfloat16),
            pltpu.VMEM((rows * SC, ny), jnp.float32),
            pltpu.VMEM((3 * co, 9 * SC), jnp.bfloat16),
            pltpu.VMEM((3 * co, 9 * co), jnp.bfloat16),
            pltpu.VMEM((2, co, ny), jnp.float32),
            pltpu.VMEM((nx * co, ny), jnp.float32),
        ],
        compiler_params=pltpu.CompilerParams(vmem_limit_bytes=48 << 20),
        name="convolutions",
    )(shot_group, *vm)


def shards(source, receiver, shot_group, w1, b1, w2, b2):
    ni, nj = lax.axis_size("shot"), lax.axis_size("slab")
    i = lax.axis_index("shot")
    pieces = cross_pieces(source, receiver, nj)
    swapped = lax.all_to_all(pieces, "slab", 0, 0, tiled=True)
    halves = swapped.reshape((-1,) + swapped.shape[2:])
    span = halves.shape[0] // ni
    here = []
    for k in range(ni):
        start = jnp.clip((i ^ k) * span - 1, 0, halves.shape[0] - span - 2)
        part = lax.dynamic_slice_in_dim(halves, start, span + 2, 0)
        here.append(part if k == 0 else lax.ppermute(part, "shot", [(a, a ^ k) for a in range(ni)]))
    place = lambda: (lax.axis_index("shot"), ni, lax.axis_index("slab"), nj)
    return convolutions(place, shot_group, here, w1, b1, w2, b2)


def solution(mesh):
    fields = P("shot", None, "slab", None, None)
    return jax.shard_map(
        shards, mesh=mesh, in_specs=(fields, fields, P(), P(), P(), P(), P()),
        out_specs=P(None, "shot", "slab", None), check_vma=False)
```

profile of v0, /device:TPU:1, one launch (start us, length us, event | category | flops | bytes accessed | tf_op | source)
XLA Modules:
  0.0 73.5 jit_solution(6872268104424081592)
XLA Ops:
  0.0 7.2 %cross.1 = bf16[32,2,3,24,128]{4,3,2,1,0:T(8,128)(2,1)} custom-call(bf16[3,8,4,256,128]{4,3,2,1,0:T(8,128)(2,1)} %src_ref.1, bf16[3,8,4,256,128]{4,3,2,1,0:T(8,128)(2,1)} %rec_ref.1), custom_call_target="tpu_custom_call" | custom-call | tf_op jit(solution)/shard_map/cross/pallas_call | solution.py:36
  7.2 0.0 copy-start.4
  7.2 9.8 %all-to-all-start = ((bf16[32,2,3,24,128]{4,3,2,1,0:T(8,128)(2,1)}), bf16[32,2,3,24,128]{4,3,2,1,0:T(8,128)(2,1)S(1)}, u32[]{:S(2)}, u32[]{:S(2)}) async-start(bf16[32,2,3,24,128]{4,3,2,1,0:T(8,128)(2,1)} %cross.1), calls=%async_computation | async-start | bytes 2359296 | tf_op jit(solution)/shard_map/all_to_all | solution.py:179
  17.1 0.0 copy-start
  17.1 0.0 copy-start.1
  17.1 0.0 copy-start.2
  17.1 0.0 copy-start.3
  17.2 18.0 %all-to-all-done = bf16[32,2,3,24,128]{4,3,2,1,0:T(8,128)(2,1)S(1)} async-done(((bf16[32,2,3,24,128]{4,3,2,1,0:T(8,128)(2,1)}), bf16[32,2,3,24,128]{4,3,2,1,0:T(8,128)(2,1)S(1)}, u32[]{:S(2)}, u32[]{:S(2)}) %all-to-all-start) | async-done | bytes 1179680 | tf_op jit(solution)/shard_map/all_to_all | solution.py:179
  35.2 0.2 constant_dynamic-slice_fusion
  35.4 4.7 %collective-permute-start.2 = (bf16[18,3,24,128]{3,2,1,0:T(8,128)(2,1)S(1)}, bf16[18,3,24,128]{3,2,1,0:T(8,128)(2,1)S(1)}, u32[]{:S(2)}, u32[]{:S(2)}) collective-permute-start(bf16[18,3,24,128]{3,2,1,0:T(8,128)(2,1)S(1)} %get-tuple-element.5), channel_id=1, source_target_pairs={{0,96},{32,64},{64,32},{96,0},{1,97},{33,65},{65,33},{97,1},{2,98}... | collective-permute-start | bytes 995336 | tf_op jit(solution)/shard_map/ppermute | solution.py:186
  40.1 0.4 collective-permute-start.1
  40.5 0.1 collective-permute-start
  40.6 0.0 copy-done.4
  40.6 0.3 copy.8
  40.9 7.8 %collective-permute-done.2.p3 = bf16[18,3,24,128]{3,2,1,0:T(8,128)(2,1)S(1)} collective-permute-done((bf16[18,3,24,128]{3,2,1,0:T(8,128)(2,1)S(1)}, bf16[18,3,24,128]{3,2,1,0:T(8,128)(2,1)S(1)}, u32[]{:S(2)}, u32[]{:S(2)}) %collective-permute-start.2) | collective-permute-done | bytes 331808 | tf_op jit(solution)/shard_map/ppermute | solution.py:186
  48.7 7.1 %collective-permute-done.1.p2 = bf16[18,3,24,128]{3,2,1,0:T(8,128)(2,1)S(1)} collective-permute-done((bf16[18,3,24,128]{3,2,1,0:T(8,128)(2,1)S(1)}, bf16[18,3,24,128]{3,2,1,0:T(8,128)(2,1)S(1)}, u32[]{:S(2)}, u32[]{:S(2)}) %collective-permute-start.1) | collective-permute-done | bytes 331808 | tf_op jit(solution)/shard_map/ppermute | solution.py:186
  55.8 0.0 collective-permute-done.p1
  55.8 0.0 copy-done
  55.8 0.0 copy-done.1
  55.8 0.0 copy-done.2
  55.8 0.0 copy-done.3
  55.8 17.7 %convolutions.1 = bf16[32,32,8,128]{3,2,1,0:T(8,128)(2,1)} custom-call(s32[12]{0:T(128)S(1)} %copy-done.1, bf16[18,3,24,128]{3,2,1,0:T(8,128)(2,1)S(1)} %get-tuple-element.8.p0, bf16[18,3,24,128]{3,2,1,0:T(8,128)(2,1)S(1)} %collective-permute-done.p1, bf16[18,3,24,128]{3,2,1,0:T(8,128)(2,1)S(1)} %collective-permute-done.1.p2, ...), custom_call_target="tpu_custom_call" | custom-call | tf_op jit(solution)/shard_map/convolutions/pallas_call | solution.py:155
Async XLA Ops:
  7.2 33.4 %copy-start.4 = (bf16[32,12,3,3,3]{0,4,3,2,1:T(4,128)(2,1)S(1)}, bf16[32,12,3,3,3]{0,4,3,2,1:T(4,128)(2,1)}, u32[]{:S(2)}) copy-start(bf16[32,12,3,3,3]{0,4,3,2,1:T(4,128)(2,1)} %param.10) | copy-start | bytes 62212
  7.2 27.9 %all-to-all-start = ((bf16[32,2,3,24,128]{4,3,2,1,0:T(8,128)(2,1)}), bf16[32,2,3,24,128]{4,3,2,1,0:T(8,128)(2,1)S(1)}, u32[]{:S(2)}, u32[]{:S(2)}) async-start(bf16[32,2,3,24,128]{4,3,2,1,0:T(8,128)(2,1)} %cross.1), calls=%async_computation | async-start | bytes 2359296 | tf_op jit(solution)/shard_map/all_to_all | solution.py:179
  17.1 38.7 %copy-start = (bf16[32,32,3,3,3]{1,0,4,3,2:T(8,128)(2,1)S(1)}, bf16[32,32,3,3,3]{1,0,4,3,2:T(8,128)(2,1)}, u32[]{:S(2)}) copy-start(bf16[32,32,3,3,3]{1,0,4,3,2:T(8,128)(2,1)} %param.12) | copy-start | bytes 165892
  17.1 38.7 %copy-start.1 = (s32[12]{0:T(128)S(1)}, s32[12]{0:T(128)}, u32[]{:S(2)}) copy-start(s32[12]{0:T(128)} %group_ref.1) | copy-start | bytes 148
  17.1 38.7 %copy-start.2 = (f32[32]{0:T(128)S(1)}, f32[32]{0:T(128)}, u32[]{:S(2)}) copy-start(f32[32]{0:T(128)} %param.11) | copy-start | bytes 388
  17.1 38.7 %copy-start.3 = (f32[32]{0:T(128)S(1)}, f32[32]{0:T(128)}, u32[]{:S(2)}) copy-start(f32[32]{0:T(128)} %param.13) | copy-start | bytes 388
  35.4 13.3 %collective-permute-start.2 = (bf16[18,3,24,128]{3,2,1,0:T(8,128)(2,1)S(1)}, bf16[18,3,24,128]{3,2,1,0:T(8,128)(2,1)S(1)}, u32[]{:S(2)}, u32[]{:S(2)}) collective-permute-start(bf16[18,3,24,128]{3,2,1,0:T(8,128)(2,1)S(1)} %get-tuple-element.5), channel_id=1, source_target_pairs={{0,96},{32,64},{64,32},{96,0},{1,97},{33,65},{65,33},{97,1},{2,98}... | collective-permute-start | bytes 995336 | tf_op jit(solution)/shard_map/ppermute | solution.py:186
  40.1 15.7 %collective-permute-start.1 = (bf16[18,3,24,128]{3,2,1,0:T(8,128)(2,1)S(1)}, bf16[18,3,24,128]{3,2,1,0:T(8,128)(2,1)S(1)}, u32[]{:S(2)}, u32[]{:S(2)}) collective-permute-start(bf16[18,3,24,128]{3,2,1,0:T(8,128)(2,1)S(1)} %get-tuple-element.6), channel_id=1, source_target_pairs={{0,64},{32,96},{64,0},{96,32},{1,65},{33,97},{65,1},{97,33},{2,66}... | collective-permute-start | bytes 995336 | tf_op jit(solution)/shard_map/ppermute | solution.py:186
  40.5 15.4 %collective-permute-start = (bf16[18,3,24,128]{3,2,1,0:T(8,128)(2,1)S(1)}, bf16[18,3,24,128]{3,2,1,0:T(8,128)(2,1)S(1)}, u32[]{:S(2)}, u32[]{:S(2)}) collective-permute-start(bf16[18,3,24,128]{3,2,1,0:T(8,128)(2,1)S(1)} %get-tuple-element.7), channel_id=1, source_target_pairs={{0,32},{32,0},{64,96},{96,64},{1,33},{33,1},{65,97},{97,65},{2,34}... | collective-permute-start | bytes 995336 | tf_op jit(solution)/shard_map/ppermute | solution.py:186
where the time goes:
time: 73.8 us; the launch traced here: 73.5 us
  waiting for transfers between devices  33 us (45%)
  Pallas kernels  24.9 us (34%)
  starting transfers between devices  15 us (20%)
    all_to_all x1, waiting for transfers between devices, shards(): swapped = lax.all_to_all(pieces, 'slab', 0, 0, tiled=True)  18 us
    pallas_call x1, Pallas kernels, convolutions(): pl.pallas_call(functools.partial(conv_kernel, place), grid=(nz // zs,), i...  17.7 us
    ppermute x3, waiting for transfers between devices, shards(): lax.ppermute(part, 'shot', [(a, a ^ k) for a in range(ni)])  14.9 us
    all_to_all x1, starting transfers between devices, shards(): swapped = lax.all_to_all(pieces, 'slab', 0, 0, tiled=True)  9.85 us
    pallas_call x1, Pallas kernels, cross_pieces(): pl.pallas_call(cross_kernel, grid=(shots, halves), in_specs=[spec, spec],...  7.23 us
    ppermute x3, starting transfers between devices, shards(): lax.ppermute(part, 'shot', [(a, a ^ k) for a in range(ni)])  5.17 us
  transfers between devices with their start and end apart: 4, of which 3 were waited for; matrix products, arithmetic and copies ran while one was open for 0% of the time, Pallas kernels for 0%

commit v1 on v0

v1 whole, which is shorter than its diff:
```python
import functools

import jax
import jax.numpy as jnp
from jax import lax
from jax.experimental import pallas as pl
from jax.experimental.pallas import tpu as pltpu
from jax.sharding import PartitionSpec as P

SC = 16

def cross_kernel(src_ref, rec_ref, out_ref, wide_ref):
    planes, nx, ny = src_ref.shape[2:]
    first = (pl.program_id(0) == 0) & (pl.program_id(1) == 0)
    edge = 2 * planes
    @pl.when(first)
    def _():
        wide_ref[0:edge, :] = jnp.zeros((edge, ny), jnp.float32)
        wide_ref[edge + planes * nx :, :] = jnp.zeros((edge, ny), jnp.float32)
    for z in range(planes):
        total = jnp.zeros((nx, ny), jnp.float32)
        for t in range(src_ref.shape[1]):
            total = total + src_ref[0, t, z].astype(jnp.float32) * rec_ref[0, t, z].astype(jnp.float32)
        wide_ref[pl.ds(edge + z, nx, stride=planes), :] = total
    rows = out_ref.shape[3]
    step = rows - 2 * edge
    for d in range(out_ref.shape[0]):
        out_ref[d, 0, 0] = wide_ref[d * step : d * step + rows, :].astype(out_ref.dtype)

def cross_pieces(source, receiver, targets):
    shots, steps, planes, nx, ny = source.shape
    halves = 2
    p = planes // halves
    rows = (nx // targets + 4) * p
    spec = pl.BlockSpec((1, steps, p, nx, ny), lambda s, h: (s, 0, h, 0, 0))
    return pl.pallas_call(
        cross_kernel,
        grid=(shots, halves),
        in_specs=[spec, spec],
        out_specs=pl.BlockSpec((targets, 1, 1, rows, ny), lambda s, h: (0, h, s, 0, 0)),
        out_shape=jax.ShapeDtypeStruct((targets, halves, shots, rows, ny), jnp.bfloat16),
        scratch_shapes=[pltpu.VMEM(((nx + 4) * p, ny), jnp.float32)],
        compiler_params=pltpu.CompilerParams(vmem_limit_bytes=48 << 20),
        name="cross",
    )(source, receiver)


def prepare_kernel(place, group_ref, w1_ref, b1_ref, w2_ref, b2_ref, k1_ref, k2_ref, bias_ref):
    co, ci = w1_ref.shape[1:]
    shots = group_ref.shape[0] // 4
    i = place()[0]
    w = k1_ref.shape[1]
    r = lax.broadcasted_iota(jnp.int32, (ci, w), 0)
    c = lax.broadcasted_iota(jnp.int32, (ci, w), 1)
    label = jnp.full((ci, w), -1, jnp.int32)
    for k in range(4):
        for s in range(shots):
            label = jnp.where(c % SC == k * shots + s, group_ref[(i ^ k) * shots + s], label)
    hit = r == label
    acc = jnp.zeros((3 * co, w), jnp.float32)
    for t in range(9):
        pick = jnp.where(hit & (c // SC == t), 1.0, 0.0).astype(jnp.bfloat16)
        left = jnp.concatenate([w1_ref[3 * t + dy] for dy in range(3)], axis=0)
        acc = acc + jnp.dot(left, pick, preferred_element_type=jnp.float32)
        for dy in range(3):
            k2_ref[dy * co : (dy + 1) * co, t * co : (t + 1) * co] = w2_ref[3 * t + dy]
    k1_ref[...] = acc.astype(jnp.bfloat16)
    eye = lax.broadcasted_iota(jnp.int32, (co, co), 0) == lax.broadcasted_iota(jnp.int32, (co, co), 1)
    for n, b in enumerate((b1_ref, b2_ref)):
        col = jnp.sum(jnp.where(eye, jnp.broadcast_to(b[...], (co, co)), 0.0), axis=1, keepdims=True)
        bias_ref[n] = jnp.broadcast_to(col, bias_ref.shape[1:])

def prepare(place, shot_group, w1, b1, w2, b2, ny):
    co, ci = w1.shape[:2]
    w1t = w1.transpose(2, 3, 4, 0, 1).reshape(27, co, ci)
    w2t = w2.transpose(2, 3, 4, 0, 1).reshape(27, co, co)
    vmem = pl.BlockSpec(memory_space=pltpu.VMEM)
    return pl.pallas_call(
        functools.partial(prepare_kernel, place),
        in_specs=[pl.BlockSpec(memory_space=pltpu.SMEM)] + [vmem] * 4,
        out_specs=[vmem] * 3,
        out_shape=[
            jax.ShapeDtypeStruct((3 * co, 9 * SC), jnp.bfloat16),
            jax.ShapeDtypeStruct((3 * co, 9 * co), jnp.bfloat16),
            jax.ShapeDtypeStruct((2, co, ny), jnp.float32),
        ],
        name="prepare",
    )(shot_group, w1t, b1.reshape(1, co), w2t, b2.reshape(1, co))

def spread(part_ref, x, bias):
    co, ny = bias.shape
    at = slice(x * ny, (x + 1) * ny)
    lane = lax.broadcasted_iota(jnp.int32, (co, ny), 1)
    low = jnp.where(lane == 0, 0.0, pltpu.roll(part_ref[:co, at], 1, 1))
    high = jnp.where(lane == ny - 1, 0.0, pltpu.roll(part_ref[2 * co :, at], ny - 1, 1))
    return jnp.maximum(part_ref[co : 2 * co, at] + low + high + bias, 0.0)

def multiply(k_ref, v_ref, z, columns, part_ref):
    ny = v_ref.shape[-1]
    for x in range(0, columns, 2):
        right = jnp.concatenate(
            [jnp.concatenate([v_ref[z + dz, x + q + dx] for dz in range(3) for dx in range(3)], axis=0) for q in range(2)], axis=1)
        part_ref[:, x * ny : (x + 2) * ny] = jnp.dot(k_ref[...], right, preferred_element_type=jnp.float32)

def conv_kernel(place, group_ref, p0, p1, p2, p3, k1_ref, k2_ref, bias_ref,
                out_ref, x_ref, h_ref, gather_ref, a0, a1, b0, b1, t0, t1):
    ny = x_ref.shape[-1]
    nhx = h_ref.shape[1]
    co, zs, nox = out_ref.shape[:3]
    nh, shots, rows = p0.shape[:3]
    per = 2
    i, ni, j, nj = place()
    parts1, parts2, turns = (a0, a1), (b0, b1), (t0, t1)

    def lay(l):
        want = l + jnp.where(i == 0, -1, jnp.where(i == ni - 1, 1, 0))
        here = jnp.clip(want, 0, nh - 1)
        keep = jnp.where((want == here) & (l < nh), 1.0, 0.0)
        for k, p in enumerate((p0, p1, p2, p3)):
            for s in range(shots):
                gather_ref[pl.ds(k * shots + s, rows, stride=SC), :] = p[here, s].astype(jnp.float32) * keep
        for x in range(rows // per):
            for z in range(per):
                at = (x * per + z) * SC
                x_ref[l * per + z, x] = gather_ref[at : at + SC, :].astype(jnp.bfloat16)

    def hide(row, part_ref, live):
        for x in range(nhx):
            v = spread(part_ref, x, bias_ref[0])
            keep = live
            if x == 0:
                keep = live & (j > 0)
            if x == nhx - 1:
                keep = live & (j < nj - 1)
            h_ref[row, x] = jnp.where(keep, v, 0.0).astype(h_ref.dtype)

    def emit(row, part_ref, turn_ref):
        for x in range(nox):
            turn_ref[pl.ds(x, co, stride=nox), :] = spread(part_ref, x, bias_ref[1])
        out_ref[:, row] = turn_ref[...].reshape(co, nox, ny).astype(out_ref.dtype)

    gather_ref[...] = jnp.zeros(gather_ref.shape, jnp.float32)
    ahead = 5
    for l in range(ahead):
        lay(l)
    for row in range(4):
        multiply(k1_ref, x_ref, row, nhx, parts1[row % 2])
        hide(row, parts1[row % 2], (i > 0) if row == 0 else (i >= 0))
    multiply(k1_ref, x_ref, 4, nhx, a1)

    @pl.when(group_ref[0] < 0)
    def _():
        for n in range(2):
            out_ref[n, 0] = parts1[n][0:nox, 0:ny].astype(out_ref.dtype)
            out_ref[n, 1] = parts2[n][0:nox, 0:ny].astype(out_ref.dtype)
            out_ref[n, 2] = turns[n][0:nox, :].astype(out_ref.dtype)
        out_ref[2, 0] = h_ref[-group_ref[0], 0, 0:nox, :]
        out_ref[3, 0] = x_ref[-group_ref[0], 0, 0:nox, :]

    @pl.loop(0, zs // 2)
    def _(p):
        for u in range(2):
            z = 2 * p + u
            multiply(k2_ref, h_ref, z, nox, parts2[u])
            multiply(k1_ref, x_ref, z + 5, nhx, parts1[u])
            hide(z + 4, parts1[1 - u], (z + 4 != zs + 1) | (i < ni - 1))
            emit(jnp.maximum(z - 1, 0), parts2[1 - u], turns[u])
        lay(p + ahead)
    emit(zs - 1, parts2[1], t0)

def convolutions(place, shot_group, pieces, w1, b1, w2, b2):
    nh, shots, rows, ny = pieces[0].shape
    nz = nh * 2 - 4
    nx = rows // 2 - 4
    co = w1.shape[0]
    k1, k2, bias = prepare(place, shot_group, w1, b1, w2, b2, ny)
    vmem = pl.BlockSpec(memory_space=pltpu.VMEM)
    f32 = jnp.float32
    return pl.pallas_call(
        functools.partial(conv_kernel, place),
        in_specs=[pl.BlockSpec(memory_space=pltpu.SMEM)] + [vmem] * 7,
        out_specs=vmem,
        out_shape=jax.ShapeDtypeStruct((co, nz, nx, ny), jnp.bfloat16),
        scratch_shapes=[
            pltpu.VMEM((nz + 10, nx + 4, SC, ny), jnp.bfloat16),
            pltpu.VMEM((nz + 4, nx + 2, co, ny), jnp.bfloat16),
            pltpu.VMEM((rows * SC, ny), f32),
            pltpu.VMEM((3 * co, (nx + 2) * ny), f32),
            pltpu.VMEM((3 * co, (nx + 2) * ny), f32),
            pltpu.VMEM((3 * co, nx * ny), f32),
            pltpu.VMEM((3 * co, nx * ny), f32),
            pltpu.VMEM((nx * co, ny), f32),
            pltpu.VMEM((nx * co, ny), f32),
        ],
        compiler_params=pltpu.CompilerParams(vmem_limit_bytes=40 << 20),
        name="convolutions",
    )(shot_group, *pieces, k1, k2, bias)

def shards(source, receiver, shot_group, w1, b1, w2, b2):
    ni, nj = lax.axis_size("shot"), lax.axis_size("slab")
    i = lax.axis_index("shot")
    pieces = cross_pieces(source, receiver, nj)
    swapped = lax.all_to_all(pieces, "slab", 0, 0, tiled=True)
    halves = swapped.reshape((-1,) + swapped.shape[2:])
    span = halves.shape[0] // ni
    here = []
    for k in range(ni):
        start = jnp.clip((i ^ k) * span - 1, 0, halves.shape[0] - span - 2)
        part = lax.dynamic_slice_in_dim(halves, start, span + 2, 0)
        here.append(part if k == 0 else lax.ppermute(part, "shot", [(a, a ^ k) for a in range(ni)]))
    place = lambda: (lax.axis_index("shot"), ni, lax.axis_index("slab"), nj)
    return convolutions(place, shot_group, here, w1, b1, w2, b2)


def solution(mesh):
    fields = P("shot", None, "slab", None, None)
    return jax.shard_map(
        shards, mesh=mesh, in_specs=(fields, fields, P(), P(), P(), P(), P()),
        out_specs=P(None, "shot", "slab", None), check_vma=False)
```

time: 73.8 us -> 71.7 us (0.972)
  local copies, waits for them, and re-layouts: 0.55 us -> 3.62 us
  Pallas kernels: 24.9 us -> 22.2 us
  waiting for transfers between devices: 33 us -> 30.4 us
    pallas_call x1 -> x2, Pallas kernels: 17.7 us -> 15 us  [the longest x1 13 us: convolutions(): pl.pallas_call(functools.partial(conv_kernel, place), in_specs=[pl.BlockS...]
    ppermute x3, waiting for transfers between devices: 14.9 us -> 12.3 us  [shards(): lax.ppermute(part, 'shot', [(a, a ^ k) for a in range(ni)])]
    unnamed x10, local copies, waits for them, and re-layouts: 0.03 us -> 2.45 us
  transfers between devices with their start and end apart: 4 -> 4, of which waited for: 3 -> 3; matrix products, arithmetic and copies ran while one was open for 0% -> 1% of each run, Pallas kernels for 0% -> 3%
where the time goes in v1:
time: 71.7 us; the launch traced here: 71.3 us
  waiting for transfers between devices  30.4 us (42%)
  Pallas kernels  22.2 us (31%)
  starting transfers between devices  15 us (21%)
  local copies, waits for them, and re-layouts  3.62 us (5%)
    all_to_all x1, waiting for transfers between devices, shards(): swapped = lax.all_to_all(pieces, 'slab', 0, 0, tiled=True)  18.1 us
    pallas_call x1, Pallas kernels, convolutions(): pl.pallas_call(functools.partial(conv_kernel, place), in_specs=[pl.BlockS...  13 us
    ppermute x3, waiting for transfers between devices, shards(): lax.ppermute(part, 'shot', [(a, a ^ k) for a in range(ni)])  12.3 us
    all_to_all x1, starting transfers between devices, shards(): swapped = lax.all_to_all(pieces, 'slab', 0, 0, tiled=True)  9.85 us
    pallas_call x1, Pallas kernels, cross_pieces(): pl.pallas_call(cross_kernel, grid=(shots, halves), in_specs=[spec, spec],...  7.23 us
    ppermute x3, starting transfers between devices, shards(): lax.ppermute(part, 'shot', [(a, a ^ k) for a in range(ni)])  5.17 us
    unnamed x10, local copies, waits for them, and re-layouts  2.45 us
    pallas_call x1, Pallas kernels, prepare(): pl.pallas_call(functools.partial(prepare_kernel, place), in_specs=[pl.Blo...  1.93 us
  transfers between devices with their start and end apart: 4, of which 3 were waited for; matrix products, arithmetic and copies ran while one was open for 1% of the time, Pallas kernels for 3%

profile of v1, /device:TPU:1, one launch (start us, length us, event | category | flops | bytes accessed | tf_op | source)
XLA Modules:
  0.0 71.3 jit_solution(12873536870899063682)
XLA Ops:
  0.0 7.2 %cross.1 = bf16[32,2,3,24,128]{4,3,2,1,0:T(8,128)(2,1)} custom-call(bf16[3,8,4,256,128]{4,3,2,1,0:T(8,128)(2,1)} %src_ref.1, bf16[3,8,4,256,128]{4,3,2,1,0:T(8,128)(2,1)} %rec_ref.1), custom_call_target="tpu_custom_call" | custom-call | tf_op jit(solution)/shard_map/cross/pallas_call | solution.py:36
  7.2 0.0 copy-start.4
  7.2 9.8 %all-to-all-start = ((bf16[32,2,3,24,128]{4,3,2,1,0:T(8,128)(2,1)}), bf16[32,2,3,24,128]{4,3,2,1,0:T(8,128)(2,1)S(1)}, u32[]{:S(2)}, u32[]{:S(2)}) async-start(bf16[32,2,3,24,128]{4,3,2,1,0:T(8,128)(2,1)} %cross.1), calls=%async_computation | async-start | bytes 2359296 | tf_op jit(solution)/shard_map/all_to_all | solution.py:203
  17.1 0.0 copy-start.3
  17.1 18.1 %all-to-all-done = bf16[32,2,3,24,128]{4,3,2,1,0:T(8,128)(2,1)S(1)} async-done(((bf16[32,2,3,24,128]{4,3,2,1,0:T(8,128)(2,1)}), bf16[32,2,3,24,128]{4,3,2,1,0:T(8,128)(2,1)S(1)}, u32[]{:S(2)}, u32[]{:S(2)}) %all-to-all-start) | async-done | bytes 1179680 | tf_op jit(solution)/shard_map/all_to_all | solution.py:203
  35.2 0.2 constant_dynamic-slice_fusion
  35.4 4.7 %collective-permute-start.2 = (bf16[18,3,24,128]{3,2,1,0:T(8,128)(2,1)S(1)}, bf16[18,3,24,128]{3,2,1,0:T(8,128)(2,1)S(1)}, u32[]{:S(2)}, u32[]{:S(2)}) collective-permute-start(bf16[18,3,24,128]{3,2,1,0:T(8,128)(2,1)S(1)} %get-tuple-element.11), channel_id=1, source_target_pairs={{0,96},{32,64},{64,32},{96,0},{1,97},{33,65},{65,33},{97,1},{2,98}... | collective-permute-start | bytes 995336 | tf_op jit(solution)/shard_map/ppermute | solution.py:210
  40.1 0.4 collective-permute-start.1
  40.5 0.1 collective-permute-start
  40.6 0.0 copy-done.4
  40.6 0.9 %copy.8 = bf16[3,3,3,32,12]{4,3,2,1,0:T(8,128)(2,1)} copy(bf16[3,3,3,32,12]{3,2,1,0,4:T(4,128)(2,1)S(1)} %bitcast.11) | data formatting | bytes 41472 | tf_op jit(solution)/shard_map/transpose | solution.py:75
  41.5 1.9 %prepare.1 = (bf16[96,144]{1,0:T(8,128)(2,1)}, bf16[96,288]{1,0:T(8,128)(2,1)}, f32[2,32,128]{2,1,0:T(8,128)}) custom-call(s32[12]{0:T(128)} %group_ref.3, bf16[27,32,12]{2,1,0:T(8,128)(2,1)} %bitcast.9, f32[1,32]{1,0:T(1,128)} %bitcast.12, bf16[27,32,32]{2,1,0:T(8,128)(2,1)} %bitcast.10, f32[1,32]{1,0:T(1,128)} %bitcast.13), custom_call_target="tpu_custom_call" | custom-call | tf_op jit(solution)/shard_map/prepare/pallas_call | solution.py:78
  43.5 5.2 %collective-permute-done.2.p3 = bf16[18,3,24,128]{3,2,1,0:T(8,128)(2,1)S(1)} collective-permute-done((bf16[18,3,24,128]{3,2,1,0:T(8,128)(2,1)S(1)}, bf16[18,3,24,128]{3,2,1,0:T(8,128)(2,1)S(1)}, u32[]{:S(2)}, u32[]{:S(2)}) %collective-permute-start.2) | collective-permute-done | bytes 331808 | tf_op jit(solution)/shard_map/ppermute | solution.py:210
  48.7 7.1 %collective-permute-done.1.p2 = bf16[18,3,24,128]{3,2,1,0:T(8,128)(2,1)S(1)} collective-permute-done((bf16[18,3,24,128]{3,2,1,0:T(8,128)(2,1)S(1)}, bf16[18,3,24,128]{3,2,1,0:T(8,128)(2,1)S(1)}, u32[]{:S(2)}, u32[]{:S(2)}) %collective-permute-start.1) | collective-permute-done | bytes 331808 | tf_op jit(solution)/shard_map/ppermute | solution.py:210
  55.8 0.0 collective-permute-done.p1
  55.8 0.0 copy-done.3
  55.8 0.0 copy-start
  55.8 0.9 %copy-done = bf16[96,288]{1,0:T(8,128)(2,1)S(1)} copy-done((bf16[96,288]{1,0:T(8,128)(2,1)S(1)}, bf16[96,288]{1,0:T(8,128)(2,1)}, u32[]{:S(2)}) %copy-start) | copy-done | bytes 55320
  56.7 0.0 copy-start.1
  56.7 0.8 %copy-done.1 = bf16[96,144]{1,0:T(8,128)(2,1)S(1)} copy-done((bf16[96,144]{1,0:T(8,128)(2,1)S(1)}, bf16[96,144]{1,0:T(8,128)(2,1)}, u32[]{:S(2)}) %copy-start.1) | copy-done | bytes 27672
  57.5 0.0 copy-start.2
  57.5 0.8 %copy-done.2 = f32[2,32,128]{2,1,0:T(8,128)S(1)} copy-done((f32[2,32,128]{2,1,0:T(8,128)S(1)}, f32[2,32,128]{2,1,0:T(8,128)}, u32[]{:S(2)}) %copy-start.2) | copy-done | bytes 32792
  58.3 13.0 %convolutions.1 = bf16[32,32,8,128]{3,2,1,0:T(8,128)(2,1)} custom-call(s32[12]{0:T(128)S(1)} %copy-done.3, bf16[18,3,24,128]{3,2,1,0:T(8,128)(2,1)S(1)} %get-tuple-element.14.p0, bf16[18,3,24,128]{3,2,1,0:T(8,128)(2,1)S(1)} %collective-permute-done.p1, bf16[18,3,24,128]{3,2,1,0:T(8,128)(2,1)S(1)} %collective-permute-done.1.p2, ...), custom_call_target="tpu_custom_call" | custom-call | tf_op jit(solution)/shard_map/convolutions/pallas_call | solution.py:179
Async XLA Ops:
  7.2 33.4 %copy-start.4 = (bf16[32,12,3,3,3]{0,4,3,2,1:T(4,128)(2,1)S(1)}, bf16[32,12,3,3,3]{0,4,3,2,1:T(4,128)(2,1)}, u32[]{:S(2)}) copy-start(bf16[32,12,3,3,3]{0,4,3,2,1:T(4,128)(2,1)} %param.10) | copy-start | bytes 62212
  7.2 27.9 %all-to-all-start = ((bf16[32,2,3,24,128]{4,3,2,1,0:T(8,128)(2,1)}), bf16[32,2,3,24,128]{4,3,2,1,0:T(8,128)(2,1)S(1)}, u32[]{:S(2)}, u32[]{:S(2)}) async-start(bf16[32,2,3,24,128]{4,3,2,1,0:T(8,128)(2,1)} %cross.1), calls=%async_computation | async-start | bytes 2359296 | tf_op jit(solution)/shard_map/all_to_all | solution.py:203
  17.1 38.7 %copy-start.3 = (s32[12]{0:T(128)S(1)}, s32[12]{0:T(128)}, u32[]{:S(2)}) copy-start(s32[12]{0:T(128)} %group_ref.3) | copy-start | bytes 148
  35.4 13.3 %collective-permute-start.2 = (bf16[18,3,24,128]{3,2,1,0:T(8,128)(2,1)S(1)}, bf16[18,3,24,128]{3,2,1,0:T(8,128)(2,1)S(1)}, u32[]{:S(2)}, u32[]{:S(2)}) collective-permute-start(bf16[18,3,24,128]{3,2,1,0:T(8,128)(2,1)S(1)} %get-tuple-element.11), channel_id=1, source_target_pairs={{0,96},{32,64},{64,32},{96,0},{1,97},{33,65},{65,33},{97,1},{2,98}... | collective-permute-start | bytes 995336 | tf_op jit(solution)/shard_map/ppermute | solution.py:210
  40.1 15.7 %collective-permute-start.1 = (bf16[18,3,24,128]{3,2,1,0:T(8,128)(2,1)S(1)}, bf16[18,3,24,128]{3,2,1,0:T(8,128)(2,1)S(1)}, u32[]{:S(2)}, u32[]{:S(2)}) collective-permute-start(bf16[18,3,24,128]{3,2,1,0:T(8,128)(2,1)S(1)} %get-tuple-element.12), channel_id=1, source_target_pairs={{0,64},{32,96},{64,0},{96,32},{1,65},{33,97},{65,1},{97,33},{2,66}... | collective-permute-start | bytes 995336 | tf_op jit(solution)/shard_map/ppermute | solution.py:210
  40.5 15.4 %collective-permute-start = (bf16[18,3,24,128]{3,2,1,0:T(8,128)(2,1)S(1)}, bf16[18,3,24,128]{3,2,1,0:T(8,128)(2,1)S(1)}, u32[]{:S(2)}, u32[]{:S(2)}) collective-permute-start(bf16[18,3,24,128]{3,2,1,0:T(8,128)(2,1)S(1)} %get-tuple-element.13), channel_id=1, source_target_pairs={{0,32},{32,0},{64,96},{96,64},{1,33},{33,1},{65,97},{97,65},{2,34}... | collective-permute-start | bytes 995336 | tf_op jit(solution)/shard_map/ppermute | solution.py:210
  55.8 0.9 %copy-start = (bf16[96,288]{1,0:T(8,128)(2,1)S(1)}, bf16[96,288]{1,0:T(8,128)(2,1)}, u32[]{:S(2)}) copy-start(bf16[96,288]{1,0:T(8,128)(2,1)} %get-tuple-element.9.k2_ref) | copy-start | bytes 165892
  56.7 0.8 %copy-start.1 = (bf16[96,144]{1,0:T(8,128)(2,1)S(1)}, bf16[96,144]{1,0:T(8,128)(2,1)}, u32[]{:S(2)}) copy-start(bf16[96,144]{1,0:T(8,128)(2,1)} %get-tuple-element.8.k1_ref) | copy-start | bytes 82948
  57.5 0.8 %copy-start.2 = (f32[2,32,128]{2,1,0:T(8,128)S(1)}, f32[2,32,128]{2,1,0:T(8,128)}, u32[]{:S(2)}) copy-start(f32[2,32,128]{2,1,0:T(8,128)} %get-tuple-element.10.bias_ref) | copy-start | bytes 98308

commit v2 on v1

--- a/solution.py
+++ b/solution.py
@@ -102,21 +102,45 @@
             [jnp.concatenate([v_ref[z + dz, x + q + dx] for dz in range(3) for dx in range(3)], axis=0) for q in range(2)], axis=1)
         part_ref[:, x * ny : (x + 2) * ny] = jnp.dot(k_ref[...], right, preferred_element_type=jnp.float32)
 
-def conv_kernel(place, group_ref, p0, p1, p2, p3, k1_ref, k2_ref, bias_ref,
-                out_ref, x_ref, h_ref, gather_ref, a0, a1, b0, b1, t0, t1):
+def conv_kernel(place, first, last, group_ref, *refs):
+    early = () if first else refs[:4]
+    refs = refs if first else refs[4:]
+    late, (k1_hbm, k2_hbm, bias_hbm), refs = refs[:4], refs[4:7], refs[7:]
+    if not first:
+        done_hbm, refs = refs[0], refs[1:]
+    (out_hbm, k1_ref, k2_ref, bias_ref, out_ref, x_ref, h_ref, gather_ref, a0, a1, b0, b1, t0, t1, sems) = refs
     ny = x_ref.shape[-1]
     nhx = h_ref.shape[1]
     co, zs, nox = out_ref.shape[:3]
-    nh, shots, rows = p0.shape[:3]
+    shots, rows = late[0].shape[1:3]
     per = 2
     i, ni, j, nj = place()
     parts1, parts2, turns = (a0, a1), (b0, b1), (t0, t1)
+    skip = 0 if first else per
+    base = out_hbm.shape[1] - zs
+
+    fetches = [pltpu.make_async_copy(src, dst, sems.at[n]) for n, (src, dst) in
+               enumerate(((k1_hbm, k1_ref), (k2_hbm, k2_ref), (bias_hbm, bias_ref)))]
+    for f in fetches:
+        f.start()
+    if not first:
+        carry = pltpu.make_async_copy(done_hbm, out_hbm.at[:, :base], sems.at[3])
+        carry.start()
 
     def lay(l):
-        want = l + jnp.where(i == 0, -1, jnp.where(i == ni - 1, 1, 0))
+        if isinstance(l, int) and l < skip:
+            source, nh = early, early[0].shape[0]
+            want = l + nh - skip - jnp.where(i == 0, 1, 0)
+        else:
+            source, nh = late, late[0].shape[0]
+            want = l - skip
+            if first:
+                want = want - jnp.where(i == 0, 1, 0)
+            if last:
+                want = want + jnp.where(i == ni - 1, 1, 0)
         here = jnp.clip(want, 0, nh - 1)
-        keep = jnp.where((want == here) & (l < nh), 1.0, 0.0)
-        for k, p in enumerate((p0, p1, p2, p3)):
+        keep = jnp.where(want == here, 1.0, 0.0)
+        for k, p in enumerate(source):
             for s in range(shots):
                 gather_ref[pl.ds(k * shots + s, rows, stride=SC), :] = p[here, s].astype(jnp.float32) * keep
         for x in range(rows // per):
@@ -143,9 +167,11 @@
     ahead = 5
     for l in range(ahead):
         lay(l)
+    for f in fetches:
+        f.wait()
     for row in range(4):
         multiply(k1_ref, x_ref, row, nhx, parts1[row % 2])
-        hide(row, parts1[row % 2], (i > 0) if row == 0 else (i >= 0))
+        hide(row, parts1[row % 2], (i > 0) if first and row == 0 else (i >= 0))
     multiply(k1_ref, x_ref, 4, nhx, a1)
 
     @pl.when(group_ref[0] < 0)
@@ -157,31 +183,54 @@
         out_ref[2, 0] = h_ref[-group_ref[0], 0, 0:nox, :]
         out_ref[3, 0] = x_ref[-group_ref[0], 0, 0:nox, :]
 
-    @pl.loop(0, zs // 2)
-    def _(p):
+    def pair(p):
         for u in range(2):
             z = 2 * p + u
             multiply(k2_ref, h_ref, z, nox, parts2[u])
             multiply(k1_ref, x_ref, z + 5, nhx, parts1[u])
-            hide(z + 4, parts1[1 - u], (z + 4 != zs + 1) | (i < ni - 1))
+            hide(z + 4, parts1[1 - u], ((z + 4 != zs + 1) | (i < ni - 1)) if last else (i >= 0))
             emit(jnp.maximum(z - 1, 0), parts2[1 - u], turns[u])
         lay(p + ahead)
+
+    pairs = zs // 2
+    cut = pairs - 3
+    ready = 2 * cut - 1
+    pl.loop(0, cut)(pair)
+    head = pltpu.make_async_copy(out_ref.at[:, :ready], out_hbm.at[:, base : base + ready], sems.at[4])
+    head.start()
+    pl.loop(cut, pairs)(pair)
     emit(zs - 1, parts2[1], t0)
-
-def convolutions(place, shot_group, pieces, w1, b1, w2, b2):
-    nh, shots, rows, ny = pieces[0].shape
-    nz = nh * 2 - 4
+    tail = pltpu.make_async_copy(out_ref.at[:, ready:], out_hbm.at[:, base + ready :], sems.at[5])
+    tail.start()
+    head.wait()
+    tail.wait()
+    if not first:
+        carry.wait()
+
+
+def convolutions(place, shot_group, early, late, done, weights, out_rows, last):
+    first = early is None
+    shots, rows, ny = late[0].shape[1:]
+    halves = late[0].shape[0] + (0 if first else 2)
+    nz = halves * 2 - 4
     nx = rows // 2 - 4
-    co = w1.shape[0]
-    k1, k2, bias = prepare(place, shot_group, w1, b1, w2, b2, ny)
+    k1, k2, bias = weights
+    co = bias.shape[1]
     vmem = pl.BlockSpec(memory_space=pltpu.VMEM)
+    hbm = pl.BlockSpec(memory_space=pl.ANY)
     f32 = jnp.float32
+    pieces = list(late) if first else list(early) + list(late)
+    more = [] if first else [done]
     return pl.pallas_call(
-        functools.partial(conv_kernel, place),
-        in_specs=[pl.BlockSpec(memory_space=pltpu.SMEM)] + [vmem] * 7,
-        out_specs=vmem,
-        out_shape=jax.ShapeDtypeStruct((co, nz, nx, ny), jnp.bfloat16),
+        functools.partial(conv_kernel, place, first, last),
+        in_specs=[pl.BlockSpec(memory_space=pltpu.SMEM)] + [vmem] * len(pieces) + [hbm] * (3 + len(more)),
+        out_specs=hbm,
+        out_shape=jax.ShapeDtypeStruct((co, out_rows, nx, ny), jnp.bfloat16),
         scratch_shapes=[
+            pltpu.VMEM(k1.shape, k1.dtype),
+            pltpu.VMEM(k2.shape, k2.dtype),
+            pltpu.VMEM(bias.shape, bias.dtype),
+            pltpu.VMEM((co, nz, nx, ny), jnp.bfloat16),
             pltpu.VMEM((nz + 10, nx + 4, SC, ny), jnp.bfloat16),
             pltpu.VMEM((nz + 4, nx + 2, co, ny), jnp.bfloat16),
             pltpu.VMEM((rows * SC, ny), f32),
@@ -191,25 +240,33 @@
             pltpu.VMEM((3 * co, nx * ny), f32),
             pltpu.VMEM((nx * co, ny), f32),
             pltpu.VMEM((nx * co, ny), f32),
+            pltpu.SemaphoreType.DMA((6,)),
         ],
-        compiler_params=pltpu.CompilerParams(vmem_limit_bytes=40 << 20),
-        name="convolutions",
-    )(shot_group, *pieces, k1, k2, bias)
+        compiler_params=pltpu.CompilerParams(vmem_limit_bytes=20 << 20),
+        name="head" if first else "tail",
+    )(shot_group, *pieces, k1, k2, bias, *more)
+
 
 def shards(source, receiver, shot_group, w1, b1, w2, b2):
     ni, nj = lax.axis_size("shot"), lax.axis_size("slab")
     i = lax.axis_index("shot")
+    place = lambda: (lax.axis_index("shot"), ni, lax.axis_index("slab"), nj)
+    weights = prepare(place, shot_group, w1, b1, w2, b2, source.shape[-1])
     pieces = cross_pieces(source, receiver, nj)
     swapped = lax.all_to_all(pieces, "slab", 0, 0, tiled=True)
     halves = swapped.reshape((-1,) + swapped.shape[2:])
     span = halves.shape[0] // ni
-    here = []
-    for k in range(ni):
-        start = jnp.clip((i ^ k) * span - 1, 0, halves.shape[0] - span - 2)
-        part = lax.dynamic_slice_in_dim(halves, start, span + 2, 0)
-        here.append(part if k == 0 else lax.ppermute(part, "shot", [(a, a ^ k) for a in range(ni)]))
-    place = lambda: (lax.axis_index("shot"), ni, lax.axis_index("slab"), nj)
-    return convolutions(place, shot_group, here, w1, b1, w2, b2)
+    chunks = []
+    for low, size in ((-1, span // 2 + 2), (span // 2 + 1, span // 2)):
+        here = []
+        for k in range(ni):
+            start = jnp.clip((i ^ k) * span + low, 0, halves.shape[0] - size)
+            part = lax.dynamic_slice_in_dim(halves, start, size, 0)
+            here.append(part if k == 0 else lax.ppermute(part, "shot", [(a, a ^ k) for a in range(ni)]))
+        chunks.append(here)
+    rows = source.shape[2] * nj // ni
+    top = convolutions(place, shot_group, None, chunks[0], None, weights, rows // 2, False)
+    return convolutions(place, shot_group, chunks[0], chunks[1], top, weights, rows, True)
 
 
 def solution(mesh):

time: 71.7 us -> 66.9 us (0.933)
  waiting for transfers between devices: 30.4 us -> 20.2 us
  starting transfers between devices: 15 us -> 18.7 us
  Pallas kernels: 22.2 us -> 23.9 us
    ppermute x3 -> x6, waiting for transfers between devices: 12.3 us -> 2.15 us  [shards(): lax.ppermute(part, 'shot', [(a, a ^ k) for a in range(ni)])]
    ppermute x3 -> x6, starting transfers between devices: 5.17 us -> 8.99 us  [shards(): lax.ppermute(part, 'shot', [(a, a ^ k) for a in range(ni)])]
    pallas_call x1 -> x2, Pallas kernels: 13 us -> 14.7 us  [convolutions(): pl.pallas_call(functools.partial(conv_kernel, place, first, last), in_spe...]
  transfers between devices with their start and end apart: 4 -> 7, of which waited for: 3 -> 3; matrix products, arithmetic and copies ran while one was open for 1% -> 2% of each run, Pallas kernels for 3% -> 14%
where the time goes in v2:
time: 66.9 us; the launch traced here: 66.4 us
  Pallas kernels  23.9 us (36%)
  waiting for transfers between devices  20.2 us (30%)
  starting transfers between devices  18.7 us (28%)
  local copies, waits for them, and re-layouts  3.53 us (5%)
    all_to_all x1, waiting for transfers between devices, shards(): swapped = lax.all_to_all(pieces, 'slab', 0, 0, tiled=True)  18.1 us
    pallas_call x2, Pallas kernels, convolutions(): pl.pallas_call(functools.partial(conv_kernel, place, first, last), in_spe...  14.7 us
    all_to_all x1, starting transfers between devices, shards(): swapped = lax.all_to_all(pieces, 'slab', 0, 0, tiled=True)  9.71 us
    ppermute x6, starting transfers between devices, shards(): lax.ppermute(part, 'shot', [(a, a ^ k) for a in range(ni)])  8.99 us
    pallas_call x1, Pallas kernels, cross_pieces(): pl.pallas_call(cross_kernel, grid=(shots, halves), in_specs=[spec, spec],...  7.23 us
    unnamed x10, local copies, waits for them, and re-layouts  2.45 us
    ppermute x6, waiting for transfers between devices, shards(): lax.ppermute(part, 'shot', [(a, a ^ k) for a in range(ni)])  2.15 us
    pallas_call x1, Pallas kernels, prepare(): pl.pallas_call(functools.partial(prepare_kernel, place), in_specs=[pl.Blo...  1.94 us
  transfers between devices with their start and end apart: 7, of which 3 were waited for; matrix products, arithmetic and copies ran while one was open for 2% of the time, Pallas kernels for 14%

profile of v2, /device:TPU:1, one launch (start us, length us, event | category | flops | bytes accessed | tf_op | source)
XLA Modules:
  0.0 66.4 jit_solution(9590684313273811607)
XLA Ops:
  0.0 7.2 %cross.1 = bf16[32,2,3,24,128]{4,3,2,1,0:T(8,128)(2,1)} custom-call(bf16[3,8,4,256,128]{4,3,2,1,0:T(8,128)(2,1)} %src_ref.1, bf16[3,8,4,256,128]{4,3,2,1,0:T(8,128)(2,1)} %rec_ref.1), custom_call_target="tpu_custom_call" | custom-call | tf_op jit(solution)/shard_map/cross/pallas_call | solution.py:36
  7.2 9.7 %all-to-all-start = ((bf16[32,2,3,24,128]{4,3,2,1,0:T(8,128)(2,1)}), bf16[32,2,3,24,128]{4,3,2,1,0:T(8,128)(2,1)S(1)}, u32[]{:S(2)}, u32[]{:S(2)}) async-start(bf16[32,2,3,24,128]{4,3,2,1,0:T(8,128)(2,1)} %cross.1), calls=%async_computation | async-start | bytes 2359296 | tf_op jit(solution)/shard_map/all_to_all | solution.py:256
  17.0 18.1 %all-to-all-done = bf16[32,2,3,24,128]{4,3,2,1,0:T(8,128)(2,1)S(1)} async-done(((bf16[32,2,3,24,128]{4,3,2,1,0:T(8,128)(2,1)}), bf16[32,2,3,24,128]{4,3,2,1,0:T(8,128)(2,1)S(1)}, u32[]{:S(2)}, u32[]{:S(2)}) %all-to-all-start) | async-done | bytes 1179680 | tf_op jit(solution)/shard_map/all_to_all | solution.py:256
  35.0 0.0 copy-start.4
  35.0 0.1 constant_dynamic-slice_fusion.4
  35.1 0.0 copy-start.3
  35.1 4.7 %collective-permute-start.2 = (bf16[10,3,24,128]{3,2,1,0:T(8,128)(2,1)S(1)}, bf16[10,3,24,128]{3,2,1,0:T(8,128)(2,1)S(1)}, u32[]{:S(2)}, u32[]{:S(2)}) collective-permute-start(bf16[10,3,24,128]{3,2,1,0:T(8,128)(2,1)S(1)} %get-tuple-element.15), channel_id=1, source_target_pairs={{0,96},{32,64},{64,32},{96,0},{1,97},{33,65},{65,33},{97,1},{2,98}... | collective-permute-start | bytes 552968 | tf_op jit(solution)/shard_map/ppermute | solution.py:265
  39.8 0.4 collective-permute-start.1
  40.2 0.2 collective-permute-start
  40.3 0.1 constant_dynamic-slice_fusion
  40.4 2.9 %collective-permute-start.5 = (bf16[8,3,24,128]{3,2,1,0:T(8,128)(2,1)S(1)}, bf16[8,3,24,128]{3,2,1,0:T(8,128)(2,1)S(1)}, u32[]{:S(2)}, u32[]{:S(2)}) collective-permute-start(bf16[8,3,24,128]{3,2,1,0:T(8,128)(2,1)S(1)} %get-tuple-element.11), channel_id=1, source_target_pairs={{0,96},{32,64},{64,32},{96,0},{1,97},{33,65},{65,33},{97,1},{2,98}... | collective-permute-start | bytes 442376 | tf_op jit(solution)/shard_map/ppermute | solution.py:265
  43.3 0.4 collective-permute-start.4
  43.7 1.6 %collective-permute-done.2.refs_3_ = bf16[10,3,24,128]{3,2,1,0:T(8,128)(2,1)S(1)} collective-permute-done((bf16[10,3,24,128]{3,2,1,0:T(8,128)(2,1)S(1)}, bf16[10,3,24,128]{3,2,1,0:T(8,128)(2,1)S(1)}, u32[]{:S(2)}, u32[]{:S(2)}) %collective-permute-start.2) | collective-permute-done | bytes 184352 | tf_op jit(solution)/shard_map/ppermute | solution.py:265
  45.3 0.5 collective-permute-start.3
  45.8 0.0 copy-done.4
  45.8 0.9 %copy.8 = bf16[3,3,3,32,12]{4,3,2,1,0:T(8,128)(2,1)} copy(bf16[3,3,3,32,12]{3,2,1,0,4:T(4,128)(2,1)S(1)} %bitcast.12) | data formatting | bytes 41472 | tf_op jit(solution)/shard_map/transpose | solution.py:75
  46.7 1.9 %prepare.1 = (bf16[96,144]{1,0:T(8,128)(2,1)}, bf16[96,288]{1,0:T(8,128)(2,1)}, f32[2,32,128]{2,1,0:T(8,128)}) custom-call(s32[12]{0:T(128)} %group_ref.5, bf16[27,32,12]{2,1,0:T(8,128)(2,1)} %bitcast.10, f32[1,32]{1,0:T(1,128)} %bitcast.13, bf16[27,32,32]{2,1,0:T(8,128)(2,1)} %bitcast.11, f32[1,32]{1,0:T(1,128)} %bitcast.14), custom_call_target="tpu_custom_call" | custom-call | tf_op jit(solution)/shard_map/prepare/pallas_call | solution.py:78
  48.6 0.6 collective-permute-done.1.refs_2_
  49.2 0.0 collective-permute-done.refs_1_
  49.2 0.0 copy-done.3
  49.2 0.0 copy-start
  49.2 0.9 %copy-done = bf16[96,288]{1,0:T(8,128)(2,1)S(1)} copy-done((bf16[96,288]{1,0:T(8,128)(2,1)S(1)}, bf16[96,288]{1,0:T(8,128)(2,1)}, u32[]{:S(2)}) %copy-start) | copy-done | bytes 55320
  50.1 0.0 copy-start.1
  50.1 0.8 %copy-done.1 = bf16[96,144]{1,0:T(8,128)(2,1)S(1)} copy-done((bf16[96,144]{1,0:T(8,128)(2,1)S(1)}, bf16[96,144]{1,0:T(8,128)(2,1)}, u32[]{:S(2)}) %copy-start.1) | copy-done | bytes 27672
  50.9 0.0 copy-start.2
  50.9 0.8 %copy-done.2 = f32[2,32,128]{2,1,0:T(8,128)S(1)} copy-done((f32[2,32,128]{2,1,0:T(8,128)S(1)}, f32[2,32,128]{2,1,0:T(8,128)}, u32[]{:S(2)}) %copy-start.2) | copy-done | bytes 32792
  51.7 7.1 %head.1.refs_11_ = bf16[32,16,8,128]{3,2,1,0:T(8,128)(2,1)S(1)} custom-call(s32[12]{0:T(128)S(1)} %copy-done.3, bf16[10,3,24,128]{3,2,1,0:T(8,128)(2,1)S(1)} %get-tuple-element.18.refs_0_, bf16[10,3,24,128]{3,2,1,0:T(8,128)(2,1)S(1)} %collective-permute-done.refs_1_, bf16[10,3,24,128]{3,2,1,0:T(8,128)(2,1)S(1)} %collective-permute-done.1.refs_2_, ...), custom_call_target="tpu_custom_call" | custom-call | tf_op jit(solution)/shard_map/head/pallas_call | solution.py:224
  58.7 0.0 collective-permute-done.5.refs_7_
  58.7 0.0 collective-permute-done.4.refs_6_
  58.8 0.0 collective-permute-done.3.refs_5_
  58.8 7.7 %tail.1 = bf16[32,32,8,128]{3,2,1,0:T(8,128)(2,1)} custom-call(s32[12]{0:T(128)S(1)} %copy-done.3, bf16[10,3,24,128]{3,2,1,0:T(8,128)(2,1)S(1)} %get-tuple-element.18.refs_0_, bf16[10,3,24,128]{3,2,1,0:T(8,128)(2,1)S(1)} %collective-permute-done.refs_1_, bf16[10,3,24,128]{3,2,1,0:T(8,128)(2,1)S(1)} %collective-permute-done.1.refs_2_, ...), custom_call_target="tpu_custom_call" | custom-call | tf_op jit(solution)/shard_map/tail/pallas_call | solution.py:224
Async XLA Ops:
  7.2 27.8 %all-to-all-start = ((bf16[32,2,3,24,128]{4,3,2,1,0:T(8,128)(2,1)}), bf16[32,2,3,24,128]{4,3,2,1,0:T(8,128)(2,1)S(1)}, u32[]{:S(2)}, u32[]{:S(2)}) async-start(bf16[32,2,3,24,128]{4,3,2,1,0:T(8,128)(2,1)} %cross.1), calls=%async_computation | async-start | bytes 2359296 | tf_op jit(solution)/shard_map/all_to_all | solution.py:256
  35.0 10.7 %copy-start.4 = (bf16[32,12,3,3,3]{0,4,3,2,1:T(4,128)(2,1)S(1)}, bf16[32,12,3,3,3]{0,4,3,2,1:T(4,128)(2,1)}, u32[]{:S(2)}) copy-start(bf16[32,12,3,3,3]{0,4,3,2,1:T(4,128)(2,1)} %param.10) | copy-start | bytes 62212
  35.1 14.1 %copy-start.3 = (s32[12]{0:T(128)S(1)}, s32[12]{0:T(128)}, u32[]{:S(2)}) copy-start(s32[12]{0:T(128)} %group_ref.5) | copy-start | bytes 148
  35.1 10.1 %collective-permute-start.2 = (bf16[10,3,24,128]{3,2,1,0:T(8,128)(2,1)S(1)}, bf16[10,3,24,128]{3,2,1,0:T(8,128)(2,1)S(1)}, u32[]{:S(2)}, u32[]{:S(2)}) collective-permute-start(bf16[10,3,24,128]{3,2,1,0:T(8,128)(2,1)S(1)} %get-tuple-element.15), channel_id=1, source_target_pairs={{0,96},{32,64},{64,32},{96,0},{1,97},{33,65},{65,33},{97,1},{2,98}... | collective-permute-start | bytes 552968 | tf_op jit(solution)/shard_map/ppermute | solution.py:265
  39.8 9.4 %collective-permute-start.1 = (bf16[10,3,24,128]{3,2,1,0:T(8,128)(2,1)S(1)}, bf16[10,3,24,128]{3,2,1,0:T(8,128)(2,1)S(1)}, u32[]{:S(2)}, u32[]{:S(2)}) collective-permute-start(bf16[10,3,24,128]{3,2,1,0:T(8,128)(2,1)S(1)} %get-tuple-element.16), channel_id=1, source_target_pairs={{0,64},{32,96},{64,0},{96,32},{1,65},{33,97},{65,1},{97,33},{2,66}... | collective-permute-start | bytes 552968 | tf_op jit(solution)/shard_map/ppermute | solution.py:265
  40.2 9.0 %collective-permute-start = (bf16[10,3,24,128]{3,2,1,0:T(8,128)(2,1)S(1)}, bf16[10,3,24,128]{3,2,1,0:T(8,128)(2,1)S(1)}, u32[]{:S(2)}, u32[]{:S(2)}) collective-permute-start(bf16[10,3,24,128]{3,2,1,0:T(8,128)(2,1)S(1)} %get-tuple-element.17), channel_id=1, source_target_pairs={{0,32},{32,0},{64,96},{96,64},{1,33},{33,1},{65,97},{97,65},{2,34}... | collective-permute-start | bytes 552968 | tf_op jit(solution)/shard_map/ppermute | solution.py:265
  40.4 18.3 %collective-permute-start.5 = (bf16[8,3,24,128]{3,2,1,0:T(8,128)(2,1)S(1)}, bf16[8,3,24,128]{3,2,1,0:T(8,128)(2,1)S(1)}, u32[]{:S(2)}, u32[]{:S(2)}) collective-permute-start(bf16[8,3,24,128]{3,2,1,0:T(8,128)(2,1)S(1)} %get-tuple-element.11), channel_id=1, source_target_pairs={{0,96},{32,64},{64,32},{96,0},{1,97},{33,65},{65,33},{97,1},{2,98}... | collective-permute-start | bytes 442376 | tf_op jit(solution)/shard_map/ppermute | solution.py:265
  43.3 15.4 %collective-permute-start.4 = (bf16[8,3,24,128]{3,2,1,0:T(8,128)(2,1)S(1)}, bf16[8,3,24,128]{3,2,1,0:T(8,128)(2,1)S(1)}, u32[]{:S(2)}, u32[]{:S(2)}) collective-permute-start(bf16[8,3,24,128]{3,2,1,0:T(8,128)(2,1)S(1)} %get-tuple-element.12), channel_id=1, source_target_pairs={{0,64},{32,96},{64,0},{96,32},{1,65},{33,97},{65,1},{97,33},{2,66}... | collective-permute-start | bytes 442376 | tf_op jit(solution)/shard_map/ppermute | solution.py:265
  45.3 13.5 %collective-permute-start.3 = (bf16[8,3,24,128]{3,2,1,0:T(8,128)(2,1)S(1)}, bf16[8,3,24,128]{3,2,1,0:T(8,128)(2,1)S(1)}, u32[]{:S(2)}, u32[]{:S(2)}) collective-permute-start(bf16[8,3,24,128]{3,2,1,0:T(8,128)(2,1)S(1)} %get-tuple-element.13), channel_id=1, source_target_pairs={{0,32},{32,0},{64,96},{96,64},{1,33},{33,1},{65,97},{97,65},{2,34}... | collective-permute-start | bytes 442376 | tf_op jit(solution)/shard_map/ppermute | solution.py:265
  49.2 0.9 %copy-start = (bf16[96,288]{1,0:T(8,128)(2,1)S(1)}, bf16[96,288]{1,0:T(8,128)(2,1)}, u32[]{:S(2)}) copy-start(bf16[96,288]{1,0:T(8,128)(2,1)} %get-tuple-element.9.refs_5_.refs_9_) | copy-start | bytes 165892
  50.1 0.8 %copy-start.1 = (bf16[96,144]{1,0:T(8,128)(2,1)S(1)}, bf16[96,144]{1,0:T(8,128)(2,1)}, u32[]{:S(2)}) copy-start(bf16[96,144]{1,0:T(8,128)(2,1)} %get-tuple-element.8.refs_4_.refs_8_) | copy-start | bytes 82948
  50.9 0.8 %copy-start.2 = (f32[2,32,128]{2,1,0:T(8,128)S(1)}, f32[2,32,128]{2,1,0:T(8,128)}, u32[]{:S(2)}) copy-start(f32[2,32,128]{2,1,0:T(8,128)} %get-tuple-element.10.refs_6_.refs_10_) | copy-start | bytes 98308

commit v3 on v2

--- a/solution.py
+++ b/solution.py
@@ -17,11 +17,14 @@
     def _():
         wide_ref[0:edge, :] = jnp.zeros((edge, ny), jnp.float32)
         wide_ref[edge + planes * nx :, :] = jnp.zeros((edge, ny), jnp.float32)
+    strip = 32
     for z in range(planes):
-        total = jnp.zeros((nx, ny), jnp.float32)
-        for t in range(src_ref.shape[1]):
-            total = total + src_ref[0, t, z].astype(jnp.float32) * rec_ref[0, t, z].astype(jnp.float32)
-        wide_ref[pl.ds(edge + z, nx, stride=planes), :] = total
+        for x in range(0, nx, strip):
+            total = None
+            for t in range(src_ref.shape[1]):
+                term = src_ref[0, t, z, x : x + strip].astype(jnp.float32) * rec_ref[0, t, z, x : x + strip].astype(jnp.float32)
+                total = term if total is None else total + term
+            wide_ref[pl.ds(edge + z + x * planes, strip, stride=planes), :] = total
     rows = out_ref.shape[3]
     step = rows - 2 * edge
     for d in range(out_ref.shape[0]):
@@ -223,7 +226,7 @@
     more = [] if first else [done]
     return pl.pallas_call(
         functools.partial(conv_kernel, place, first, last),
-        in_specs=[pl.BlockSpec(memory_space=pltpu.SMEM)] + [vmem] * len(pieces) + [hbm] * (3 + len(more)),
+        in_specs=[pl.BlockSpec(memory_space=pltpu.SMEM)] + [vmem] * len(pieces) + [pl.BlockSpec(memory_space=pltpu.HBM)] * 3 + [hbm] * len(more),
         out_specs=hbm,
         out_shape=jax.ShapeDtypeStruct((co, out_rows, nx, ny), jnp.bfloat16),
         scratch_shapes=[

time: 66.9 us -> 66.5 us (level)
  no operation moved by 1% of the time
where the time goes in v3:
time: 66.5 us; the launch traced here: 66.1 us
  Pallas kernels  23.5 us (35%)
  waiting for transfers between devices  20.2 us (30%)
  starting transfers between devices  18.7 us (28%)
  local copies, waits for them, and re-layouts  3.53 us (5%)
    all_to_all x1, waiting for transfers between devices, shards(): swapped = lax.all_to_all(pieces, 'slab', 0, 0, tiled=True)  18.1 us
    pallas_call x2, Pallas kernels, convolutions(): pl.pallas_call(functools.partial(conv_kernel, place, first, last), in_spe...  14.8 us
    all_to_all x1, starting transfers between devices, shards(): swapped = lax.all_to_all(pieces, 'slab', 0, 0, tiled=True)  9.71 us
    ppermute x6, starting transfers between devices, shards(): lax.ppermute(part, 'shot', [(a, a ^ k) for a in range(ni)])  8.99 us
    pallas_call x1, Pallas kernels, cross_pieces(): pl.pallas_call(cross_kernel, grid=(shots, halves), in_specs=[spec, spec],...  6.86 us
    unnamed x10, local copies, waits for them, and re-layouts  2.45 us
    ppermute x6, waiting for transfers between devices, shards(): lax.ppermute(part, 'shot', [(a, a ^ k) for a in range(ni)])  2.15 us
    pallas_call x1, Pallas kernels, prepare(): pl.pallas_call(functools.partial(prepare_kernel, place), in_specs=[pl.Blo...  1.94 us
  transfers between devices with their start and end apart: 7, of which 3 were waited for; matrix products, arithmetic and copies ran while one was open for 2% of the time, Pallas kernels for 14%

profile of v3, /device:TPU:1, one launch (start us, length us, event | category | flops | bytes accessed | tf_op | source)
XLA Modules:
  0.0 66.1 jit_solution(8620726882468495629)
XLA Ops:
  0.0 6.9 %cross.1 = bf16[32,2,3,24,128]{4,3,2,1,0:T(8,128)(2,1)} custom-call(bf16[3,8,4,256,128]{4,3,2,1,0:T(8,128)(2,1)} %src_ref.1, bf16[3,8,4,256,128]{4,3,2,1,0:T(8,128)(2,1)} %rec_ref.1), custom_call_target="tpu_custom_call" | custom-call | tf_op jit(solution)/shard_map/cross/pallas_call | solution.py:39
  6.9 9.7 %all-to-all-start = ((bf16[32,2,3,24,128]{4,3,2,1,0:T(8,128)(2,1)}), bf16[32,2,3,24,128]{4,3,2,1,0:T(8,128)(2,1)S(1)}, u32[]{:S(2)}, u32[]{:S(2)}) async-start(bf16[32,2,3,24,128]{4,3,2,1,0:T(8,128)(2,1)} %cross.1), calls=%async_computation | async-start | bytes 2359296 | tf_op jit(solution)/shard_map/all_to_all | solution.py:259
  16.6 18.1 %all-to-all-done = bf16[32,2,3,24,128]{4,3,2,1,0:T(8,128)(2,1)S(1)} async-done(((bf16[32,2,3,24,128]{4,3,2,1,0:T(8,128)(2,1)}), bf16[32,2,3,24,128]{4,3,2,1,0:T(8,128)(2,1)S(1)}, u32[]{:S(2)}, u32[]{:S(2)}) %all-to-all-start) | async-done | bytes 1179680 | tf_op jit(solution)/shard_map/all_to_all | solution.py:259
  34.7 0.0 copy-start.4
  34.7 0.1 constant_dynamic-slice_fusion.4
  34.8 0.0 copy-start.3
  34.8 4.7 %collective-permute-start.2 = (bf16[10,3,24,128]{3,2,1,0:T(8,128)(2,1)S(1)}, bf16[10,3,24,128]{3,2,1,0:T(8,128)(2,1)S(1)}, u32[]{:S(2)}, u32[]{:S(2)}) collective-permute-start(bf16[10,3,24,128]{3,2,1,0:T(8,128)(2,1)S(1)} %get-tuple-element.15), channel_id=1, source_target_pairs={{0,96},{32,64},{64,32},{96,0},{1,97},{33,65},{65,33},{97,1},{2,98}... | collective-permute-start | bytes 552968 | tf_op jit(solution)/shard_map/ppermute | solution.py:268
  39.5 0.4 collective-permute-start.1
  39.8 0.2 collective-permute-start
  40.0 0.1 constant_dynamic-slice_fusion
  40.0 2.9 %collective-permute-start.5 = (bf16[8,3,24,128]{3,2,1,0:T(8,128)(2,1)S(1)}, bf16[8,3,24,128]{3,2,1,0:T(8,128)(2,1)S(1)}, u32[]{:S(2)}, u32[]{:S(2)}) collective-permute-start(bf16[8,3,24,128]{3,2,1,0:T(8,128)(2,1)S(1)} %get-tuple-element.11), channel_id=1, source_target_pairs={{0,96},{32,64},{64,32},{96,0},{1,97},{33,65},{65,33},{97,1},{2,98}... | collective-permute-start | bytes 442376 | tf_op jit(solution)/shard_map/ppermute | solution.py:268
  43.0 0.4 collective-permute-start.4
  43.3 1.6 %collective-permute-done.2.refs_3_ = bf16[10,3,24,128]{3,2,1,0:T(8,128)(2,1)S(1)} collective-permute-done((bf16[10,3,24,128]{3,2,1,0:T(8,128)(2,1)S(1)}, bf16[10,3,24,128]{3,2,1,0:T(8,128)(2,1)S(1)}, u32[]{:S(2)}, u32[]{:S(2)}) %collective-permute-start.2) | collective-permute-done | bytes 184352 | tf_op jit(solution)/shard_map/ppermute | solution.py:268
  44.9 0.5 collective-permute-start.3
  45.4 0.0 copy-done.4
  45.4 0.9 %copy.8 = bf16[3,3,3,32,12]{4,3,2,1,0:T(8,128)(2,1)} copy(bf16[3,3,3,32,12]{3,2,1,0,4:T(4,128)(2,1)S(1)} %bitcast.12) | data formatting | bytes 41472 | tf_op jit(solution)/shard_map/transpose | solution.py:78
  46.3 1.9 %prepare.1 = (bf16[96,144]{1,0:T(8,128)(2,1)}, bf16[96,288]{1,0:T(8,128)(2,1)}, f32[2,32,128]{2,1,0:T(8,128)}) custom-call(s32[12]{0:T(128)} %group_ref.5, bf16[27,32,12]{2,1,0:T(8,128)(2,1)} %bitcast.10, f32[1,32]{1,0:T(1,128)} %bitcast.13, bf16[27,32,32]{2,1,0:T(8,128)(2,1)} %bitcast.11, f32[1,32]{1,0:T(1,128)} %bitcast.14), custom_call_target="tpu_custom_call" | custom-call | tf_op jit(solution)/shard_map/prepare/pallas_call | solution.py:81
  48.3 0.6 collective-permute-done.1.refs_2_
  48.8 0.0 collective-permute-done.refs_1_
  48.9 0.0 copy-done.3
  48.9 0.0 copy-start
  48.9 0.9 %copy-done = bf16[96,288]{1,0:T(8,128)(2,1)S(1)} copy-done((bf16[96,288]{1,0:T(8,128)(2,1)S(1)}, bf16[96,288]{1,0:T(8,128)(2,1)}, u32[]{:S(2)}) %copy-start) | copy-done | bytes 55320
  49.7 0.0 copy-start.1
  49.7 0.8 %copy-done.1 = bf16[96,144]{1,0:T(8,128)(2,1)S(1)} copy-done((bf16[96,144]{1,0:T(8,128)(2,1)S(1)}, bf16[96,144]{1,0:T(8,128)(2,1)}, u32[]{:S(2)}) %copy-start.1) | copy-done | bytes 27672
  50.5 0.0 copy-start.2
  50.5 0.8 %copy-done.2 = f32[2,32,128]{2,1,0:T(8,128)S(1)} copy-done((f32[2,32,128]{2,1,0:T(8,128)S(1)}, f32[2,32,128]{2,1,0:T(8,128)}, u32[]{:S(2)}) %copy-start.2) | copy-done | bytes 32792
  51.3 7.1 %head.1.refs_11_ = bf16[32,16,8,128]{3,2,1,0:T(8,128)(2,1)S(1)} custom-call(s32[12]{0:T(128)S(1)} %copy-done.3, bf16[10,3,24,128]{3,2,1,0:T(8,128)(2,1)S(1)} %get-tuple-element.18.refs_0_, bf16[10,3,24,128]{3,2,1,0:T(8,128)(2,1)S(1)} %collective-permute-done.refs_1_, bf16[10,3,24,128]{3,2,1,0:T(8,128)(2,1)S(1)} %collective-permute-done.1.refs_2_, ...), custom_call_target="tpu_custom_call" | custom-call | tf_op jit(solution)/shard_map/head/pallas_call | solution.py:227
  58.4 0.0 collective-permute-done.5.refs_7_
  58.4 0.0 collective-permute-done.4.refs_6_
  58.4 0.0 collective-permute-done.3.refs_5_
  58.4 7.7 %tail.1 = bf16[32,32,8,128]{3,2,1,0:T(8,128)(2,1)} custom-call(s32[12]{0:T(128)S(1)} %copy-done.3, bf16[10,3,24,128]{3,2,1,0:T(8,128)(2,1)S(1)} %get-tuple-element.18.refs_0_, bf16[10,3,24,128]{3,2,1,0:T(8,128)(2,1)S(1)} %collective-permute-done.refs_1_, bf16[10,3,24,128]{3,2,1,0:T(8,128)(2,1)S(1)} %collective-permute-done.1.refs_2_, ...), custom_call_target="tpu_custom_call" | custom-call | tf_op jit(solution)/shard_map/tail/pallas_call | solution.py:227
Async XLA Ops:
  6.9 27.8 %all-to-all-start = ((bf16[32,2,3,24,128]{4,3,2,1,0:T(8,128)(2,1)}), bf16[32,2,3,24,128]{4,3,2,1,0:T(8,128)(2,1)S(1)}, u32[]{:S(2)}, u32[]{:S(2)}) async-start(bf16[32,2,3,24,128]{4,3,2,1,0:T(8,128)(2,1)} %cross.1), calls=%async_computation | async-start | bytes 2359296 | tf_op jit(solution)/shard_map/all_to_all | solution.py:259
  34.7 10.7 %copy-start.4 = (bf16[32,12,3,3,3]{0,4,3,2,1:T(4,128)(2,1)S(1)}, bf16[32,12,3,3,3]{0,4,3,2,1:T(4,128)(2,1)}, u32[]{:S(2)}) copy-start(bf16[32,12,3,3,3]{0,4,3,2,1:T(4,128)(2,1)} %param.10) | copy-start | bytes 62212
  34.8 14.1 %copy-start.3 = (s32[12]{0:T(128)S(1)}, s32[12]{0:T(128)}, u32[]{:S(2)}) copy-start(s32[12]{0:T(128)} %group_ref.5) | copy-start | bytes 148
  34.8 10.1 %collective-permute-start.2 = (bf16[10,3,24,128]{3,2,1,0:T(8,128)(2,1)S(1)}, bf16[10,3,24,128]{3,2,1,0:T(8,128)(2,1)S(1)}, u32[]{:S(2)}, u32[]{:S(2)}) collective-permute-start(bf16[10,3,24,128]{3,2,1,0:T(8,128)(2,1)S(1)} %get-tuple-element.15), channel_id=1, source_target_pairs={{0,96},{32,64},{64,32},{96,0},{1,97},{33,65},{65,33},{97,1},{2,98}... | collective-permute-start | bytes 552968 | tf_op jit(solution)/shard_map/ppermute | solution.py:268
  39.5 9.4 %collective-permute-start.1 = (bf16[10,3,24,128]{3,2,1,0:T(8,128)(2,1)S(1)}, bf16[10,3,24,128]{3,2,1,0:T(8,128)(2,1)S(1)}, u32[]{:S(2)}, u32[]{:S(2)}) collective-permute-start(bf16[10,3,24,128]{3,2,1,0:T(8,128)(2,1)S(1)} %get-tuple-element.16), channel_id=1, source_target_pairs={{0,64},{32,96},{64,0},{96,32},{1,65},{33,97},{65,1},{97,33},{2,66}... | collective-permute-start | bytes 552968 | tf_op jit(solution)/shard_map/ppermute | solution.py:268
  39.8 9.0 %collective-permute-start = (bf16[10,3,24,128]{3,2,1,0:T(8,128)(2,1)S(1)}, bf16[10,3,24,128]{3,2,1,0:T(8,128)(2,1)S(1)}, u32[]{:S(2)}, u32[]{:S(2)}) collective-permute-start(bf16[10,3,24,128]{3,2,1,0:T(8,128)(2,1)S(1)} %get-tuple-element.17), channel_id=1, source_target_pairs={{0,32},{32,0},{64,96},{96,64},{1,33},{33,1},{65,97},{97,65},{2,34}... | collective-permute-start | bytes 552968 | tf_op jit(solution)/shard_map/ppermute | solution.py:268
  40.0 18.3 %collective-permute-start.5 = (bf16[8,3,24,128]{3,2,1,0:T(8,128)(2,1)S(1)}, bf16[8,3,24,128]{3,2,1,0:T(8,128)(2,1)S(1)}, u32[]{:S(2)}, u32[]{:S(2)}) collective-permute-start(bf16[8,3,24,128]{3,2,1,0:T(8,128)(2,1)S(1)} %get-tuple-element.11), channel_id=1, source_target_pairs={{0,96},{32,64},{64,32},{96,0},{1,97},{33,65},{65,33},{97,1},{2,98}... | collective-permute-start | bytes 442376 | tf_op jit(solution)/shard_map/ppermute | solution.py:268
  43.0 15.4 %collective-permute-start.4 = (bf16[8,3,24,128]{3,2,1,0:T(8,128)(2,1)S(1)}, bf16[8,3,24,128]{3,2,1,0:T(8,128)(2,1)S(1)}, u32[]{:S(2)}, u32[]{:S(2)}) collective-permute-start(bf16[8,3,24,128]{3,2,1,0:T(8,128)(2,1)S(1)} %get-tuple-element.12), channel_id=1, source_target_pairs={{0,64},{32,96},{64,0},{96,32},{1,65},{33,97},{65,1},{97,33},{2,66}... | collective-permute-start | bytes 442376 | tf_op jit(solution)/shard_map/ppermute | solution.py:268
  44.9 13.5 %collective-permute-start.3 = (bf16[8,3,24,128]{3,2,1,0:T(8,128)(2,1)S(1)}, bf16[8,3,24,128]{3,2,1,0:T(8,128)(2,1)S(1)}, u32[]{:S(2)}, u32[]{:S(2)}) collective-permute-start(bf16[8,3,24,128]{3,2,1,0:T(8,128)(2,1)S(1)} %get-tuple-element.13), channel_id=1, source_target_pairs={{0,32},{32,0},{64,96},{96,64},{1,33},{33,1},{65,97},{97,65},{2,34}... | collective-permute-start | bytes 442376 | tf_op jit(solution)/shard_map/ppermute | solution.py:268
  48.9 0.9 %copy-start = (bf16[96,288]{1,0:T(8,128)(2,1)S(1)}, bf16[96,288]{1,0:T(8,128)(2,1)}, u32[]{:S(2)}) copy-start(bf16[96,288]{1,0:T(8,128)(2,1)} %get-tuple-element.9.refs_5_.refs_9_) | copy-start | bytes 165892
  49.7 0.8 %copy-start.1 = (bf16[96,144]{1,0:T(8,128)(2,1)S(1)}, bf16[96,144]{1,0:T(8,128)(2,1)}, u32[]{:S(2)}) copy-start(bf16[96,144]{1,0:T(8,128)(2,1)} %get-tuple-element.8.refs_4_.refs_8_) | copy-start | bytes 82948
  50.5 0.8 %copy-start.2 = (f32[2,32,128]{2,1,0:T(8,128)S(1)}, f32[2,32,128]{2,1,0:T(8,128)}, u32[]{:S(2)}) copy-start(f32[2,32,128]{2,1,0:T(8,128)} %get-tuple-element.10.refs_6_.refs_10_) | copy-start | bytes 98308

commit v4 on v3

--- a/solution.py
+++ b/solution.py
@@ -60,14 +60,18 @@
         for s in range(shots):
             label = jnp.where(c % SC == k * shots + s, group_ref[(i ^ k) * shots + s], label)
     hit = r == label
-    acc = jnp.zeros((3 * co, w), jnp.float32)
-    for t in range(9):
-        pick = jnp.where(hit & (c // SC == t), 1.0, 0.0).astype(jnp.bfloat16)
-        left = jnp.concatenate([w1_ref[3 * t + dy] for dy in range(3)], axis=0)
-        acc = acc + jnp.dot(left, pick, preferred_element_type=jnp.float32)
-        for dy in range(3):
-            k2_ref[dy * co : (dy + 1) * co, t * co : (t + 1) * co] = w2_ref[3 * t + dy]
-    k1_ref[...] = acc.astype(jnp.bfloat16)
+    k2_ref[...] = jnp.zeros(k2_ref.shape, k2_ref.dtype)
+    for oz in range(2):
+        acc = jnp.zeros((3 * co, w), jnp.float32)
+        for t in range(9):
+            column = 3 * oz + t
+            pick = jnp.where(hit & (c // SC == column), 1.0, 0.0).astype(jnp.bfloat16)
+            left = jnp.concatenate([w1_ref[3 * t + dy] for dy in range(3)], axis=0)
+            acc = acc + jnp.dot(left, pick, preferred_element_type=jnp.float32)
+            for dy in range(3):
+                row = (3 * oz + dy) * co
+                k2_ref[row : row + co, column * co : (column + 1) * co] = w2_ref[3 * t + dy]
+        k1_ref[3 * oz * co : 3 * (oz + 1) * co, :] = acc.astype(jnp.bfloat16)
     eye = lax.broadcasted_iota(jnp.int32, (co, co), 0) == lax.broadcasted_iota(jnp.int32, (co, co), 1)
     for n, b in enumerate((b1_ref, b2_ref)):
         col = jnp.sum(jnp.where(eye, jnp.broadcast_to(b[...], (co, co)), 0.0), axis=1, keepdims=True)
@@ -83,26 +87,27 @@
         in_specs=[pl.BlockSpec(memory_space=pltpu.SMEM)] + [vmem] * 4,
         out_specs=[vmem] * 3,
         out_shape=[
-            jax.ShapeDtypeStruct((3 * co, 9 * SC), jnp.bfloat16),
-            jax.ShapeDtypeStruct((3 * co, 9 * co), jnp.bfloat16),
+            jax.ShapeDtypeStruct((6 * co, 12 * SC), jnp.bfloat16),
+            jax.ShapeDtypeStruct((6 * co, 12 * co), jnp.bfloat16),
             jax.ShapeDtypeStruct((2, co, ny), jnp.float32),
         ],
         name="prepare",
     )(shot_group, w1t, b1.reshape(1, co), w2t, b2.reshape(1, co))
 
-def spread(part_ref, x, bias):
+def spread(part_ref, oz, x, bias):
     co, ny = bias.shape
     at = slice(x * ny, (x + 1) * ny)
+    low_at, mid_at, high_at = (slice((3 * oz + n) * co, (3 * oz + n + 1) * co) for n in range(3))
     lane = lax.broadcasted_iota(jnp.int32, (co, ny), 1)
-    low = jnp.where(lane == 0, 0.0, pltpu.roll(part_ref[:co, at], 1, 1))
-    high = jnp.where(lane == ny - 1, 0.0, pltpu.roll(part_ref[2 * co :, at], ny - 1, 1))
-    return jnp.maximum(part_ref[co : 2 * co, at] + low + high + bias, 0.0)
+    low = jnp.where(lane == 0, 0.0, pltpu.roll(part_ref[low_at, at], 1, 1))
+    high = jnp.where(lane == ny - 1, 0.0, pltpu.roll(part_ref[high_at, at], ny - 1, 1))
+    return jnp.maximum(part_ref[mid_at, at] + low + high + bias, 0.0)
 
 def multiply(k_ref, v_ref, z, columns, part_ref):
     ny = v_ref.shape[-1]
     for x in range(0, columns, 2):
         right = jnp.concatenate(
-            [jnp.concatenate([v_ref[z + dz, x + q + dx] for dz in range(3) for dx in range(3)], axis=0) for q in range(2)], axis=1)
+            [jnp.concatenate([v_ref[z + dz, x + q + dx] for dz in range(4) for dx in range(3)], axis=0) for q in range(2)], axis=1)
         part_ref[:, x * ny : (x + 2) * ny] = jnp.dot(k_ref[...], right, preferred_element_type=jnp.float32)
 
 def conv_kernel(place, first, last, group_ref, *refs):
@@ -151,20 +156,23 @@
                 at = (x * per + z) * SC
                 x_ref[l * per + z, x] = gather_ref[at : at + SC, :].astype(jnp.bfloat16)
 
-    def hide(row, part_ref, live):
-        for x in range(nhx):
-            v = spread(part_ref, x, bias_ref[0])
-            keep = live
-            if x == 0:
-                keep = live & (j > 0)
-            if x == nhx - 1:
-                keep = live & (j < nj - 1)
-            h_ref[row, x] = jnp.where(keep, v, 0.0).astype(h_ref.dtype)
-
-    def emit(row, part_ref, turn_ref):
-        for x in range(nox):
-            turn_ref[pl.ds(x, co, stride=nox), :] = spread(part_ref, x, bias_ref[1])
-        out_ref[:, row] = turn_ref[...].reshape(co, nox, ny).astype(out_ref.dtype)
+    def hide(pair, part_ref, lives):
+        for oz in range(2):
+            for x in range(nhx):
+                v = spread(part_ref, oz, x, bias_ref[0])
+                keep = lives[oz]
+                if x == 0:
+                    keep = keep & (j > 0)
+                if x == nhx - 1:
+                    keep = keep & (j < nj - 1)
+                h_ref[2 * pair + oz, x] = jnp.where(keep, v, 0.0).astype(h_ref.dtype)
+
+    def emit(pair, part_ref):
+        for oz in range(2):
+            turn_ref = turns[oz]
+            for x in range(nox):
+                turn_ref[pl.ds(x, co, stride=nox), :] = spread(part_ref, oz, x, bias_ref[1])
+            out_ref[:, 2 * pair + oz] = turn_ref[...].reshape(co, nox, ny).astype(out_ref.dtype)
 
     gather_ref[...] = jnp.zeros(gather_ref.shape, jnp.float32)
     ahead = 5
@@ -172,9 +180,10 @@
         lay(l)
     for f in fetches:
         f.wait()
-    for row in range(4):
-        multiply(k1_ref, x_ref, row, nhx, parts1[row % 2])
-        hide(row, parts1[row % 2], (i > 0) if first and row == 0 else (i >= 0))
+    always = i >= 0
+    for pair in range(2):
+        multiply(k1_ref, x_ref, 2 * pair, nhx, parts1[pair])
+        hide(pair, parts1[pair], ((i > 0) if first and pair == 0 else always, always))
     multiply(k1_ref, x_ref, 4, nhx, a1)
 
     @pl.when(group_ref[0] < 0)
@@ -186,23 +195,23 @@
         out_ref[2, 0] = h_ref[-group_ref[0], 0, 0:nox, :]
         out_ref[3, 0] = x_ref[-group_ref[0], 0, 0:nox, :]
 
-    def pair(p):
+    def quad(n):
         for u in range(2):
-            z = 2 * p + u
-            multiply(k2_ref, h_ref, z, nox, parts2[u])
-            multiply(k1_ref, x_ref, z + 5, nhx, parts1[u])
-            hide(z + 4, parts1[1 - u], ((z + 4 != zs + 1) | (i < ni - 1)) if last else (i >= 0))
-            emit(jnp.maximum(z - 1, 0), parts2[1 - u], turns[u])
-        lay(p + ahead)
-
-    pairs = zs // 2
-    cut = pairs - 3
-    ready = 2 * cut - 1
-    pl.loop(0, cut)(pair)
+            p = 2 * n + u
+            multiply(k2_ref, h_ref, 2 * p, nox, parts2[u])
+            multiply(k1_ref, x_ref, 2 * p + 6, nhx, parts1[u])
+            hide(p + 2, parts1[1 - u], (always, ((2 * p + 5 != zs + 1) | (i < ni - 1)) if last else always))
+            emit(jnp.maximum(p - 1, 0), parts2[1 - u])
+            lay(p + ahead)
+
+    quads = zs // 4
+    cut = quads - 1
+    ready = 2 * (2 * cut - 1)
+    pl.loop(0, cut)(quad)
     head = pltpu.make_async_copy(out_ref.at[:, :ready], out_hbm.at[:, base : base + ready], sems.at[4])
     head.start()
-    pl.loop(cut, pairs)(pair)
-    emit(zs - 1, parts2[1], t0)
+    pl.loop(cut, quads)(quad)
+    emit(zs // 2 - 1, parts2[1])
     tail = pltpu.make_async_copy(out_ref.at[:, ready:], out_hbm.at[:, base + ready :], sems.at[5])
     tail.start()
     head.wait()
@@ -237,10 +246,10 @@
             pltpu.VMEM((nz + 10, nx + 4, SC, ny), jnp.bfloat16),
             pltpu.VMEM((nz + 4, nx + 2, co, ny), jnp.bfloat16),
             pltpu.VMEM((rows * SC, ny), f32),
-            pltpu.VMEM((3 * co, (nx + 2) * ny), f32),
-            pltpu.VMEM((3 * co, (nx + 2) * ny), f32),
-            pltpu.VMEM((3 * co, nx * ny), f32),
-            pltpu.VMEM((3 * co, nx * ny), f32),
+            pltpu.VMEM((6 * co, (nx + 2) * ny), f32),
+            pltpu.VMEM((6 * co, (nx + 2) * ny), f32),
+            pltpu.VMEM((6 * co, nx * ny), f32),
+            pltpu.VMEM((6 * co, nx * ny), f32),
             pltpu.VMEM((nx * co, ny), f32),
             pltpu.VMEM((nx * co, ny), f32),
             pltpu.SemaphoreType.DMA((6,)),
@@ -257,6 +266,7 @@
     weights = prepare(place, shot_group, w1, b1, w2, b2, source.shape[-1])
     pieces = cross_pieces(source, receiver, nj)
     swapped = lax.all_to_all(pieces, "slab", 0, 0, tiled=True)
+    swapped, weights = lax.optimization_barrier((swapped, weights))
     halves = swapped.reshape((-1,) + swapped.shape[2:])
     span = halves.shape[0] // ni
     chunks = []

time: 66.5 us -> 62.5 us (0.940)
  local copies, waits for them, and re-layouts: 3.53 us -> 1.11 us
  Pallas kernels: 23.5 us -> 22.1 us
    all_to_all x1, waiting for transfers between devices: 18.1 us -> 15 us  [shards(): swapped = lax.all_to_all(pieces, 'slab', 0, 0, tiled=True)]
    ppermute x6, waiting for transfers between devices: 2.15 us -> 5.03 us  [shards(): lax.ppermute(part, 'shot', [(a, a ^ k) for a in range(ni)])]
    unnamed x10, local copies, waits for them, and re-layouts: 2.45 us -> 0.02 us
    pallas_call x2, Pallas kernels: 14.8 us -> 13.2 us  [convolutions(): pl.pallas_call(functools.partial(conv_kernel, place, first, last), in_spe...]
  transfers between devices with their start and end apart: 7 -> 7, of which waited for: 3 -> 3; matrix products, arithmetic and copies ran while one was open for 2% -> 2% of each run, Pallas kernels for 14% -> 13%
where the time goes in v4:
time: 62.5 us; the launch traced here: 62.2 us
  Pallas kernels  22.1 us (35%)
  waiting for transfers between devices  20.1 us (32%)
  starting transfers between devices  18.8 us (30%)
  local copies, waits for them, and re-layouts  1.11 us (2%)
    all_to_all x1, waiting for transfers between devices, shards(): swapped = lax.all_to_all(pieces, 'slab', 0, 0, tiled=True)  15 us
    pallas_call x2, Pallas kernels, convolutions(): pl.pallas_call(functools.partial(conv_kernel, place, first, last), in_spe...  13.2 us
    all_to_all x1, starting transfers between devices, shards(): swapped = lax.all_to_all(pieces, 'slab', 0, 0, tiled=True)  9.85 us
    ppermute x6, starting transfers between devices, shards(): lax.ppermute(part, 'shot', [(a, a ^ k) for a in range(ni)])  8.99 us
    pallas_call x1, Pallas kernels, cross_pieces(): pl.pallas_call(cross_kernel, grid=(shots, halves), in_specs=[spec, spec],...  6.86 us
    ppermute x6, waiting for transfers between devices, shards(): lax.ppermute(part, 'shot', [(a, a ^ k) for a in range(ni)])  5.03 us
    pallas_call x1, Pallas kernels, prepare(): pl.pallas_call(functools.partial(prepare_kernel, place), in_specs=[pl.Blo...  2.07 us
  transfers between devices with their start and end apart: 7, of which 3 were waited for; matrix products, arithmetic and copies ran while one was open for 2% of the time, Pallas kernels for 13%

profile of v4, /device:TPU:1, one launch (start us, length us, event | category | flops | bytes accessed | tf_op | source)
XLA Modules:
  0.0 62.2 jit_solution(10845503682489260442)
XLA Ops:
  0.0 6.9 %cross.1 = bf16[32,2,3,24,128]{4,3,2,1,0:T(8,128)(2,1)} custom-call(bf16[3,8,4,256,128]{4,3,2,1,0:T(8,128)(2,1)} %src_ref.1, bf16[3,8,4,256,128]{4,3,2,1,0:T(8,128)(2,1)} %rec_ref.1), custom_call_target="tpu_custom_call" | custom-call | tf_op jit(solution)/shard_map/cross/pallas_call | solution.py:39
  6.9 0.0 copy-start.4
  6.9 9.8 %all-to-all-start = ((bf16[32,2,3,24,128]{4,3,2,1,0:T(8,128)(2,1)}), bf16[32,2,3,24,128]{4,3,2,1,0:T(8,128)(2,1)S(1)}, u32[]{:S(2)}, u32[]{:S(2)}) async-start(bf16[32,2,3,24,128]{4,3,2,1,0:T(8,128)(2,1)} %cross.1), calls=%async_computation | async-start | bytes 2359296 | tf_op jit(solution)/shard_map/all_to_all | solution.py:268
  16.7 0.0 copy-done.4
  16.8 0.9 %copy.8 = bf16[3,3,3,32,12]{4,3,2,1,0:T(8,128)(2,1)} copy(bf16[3,3,3,32,12]{3,2,1,0,4:T(4,128)(2,1)S(1)} %bitcast.12) | data formatting | bytes 41472 | tf_op jit(solution)/shard_map/transpose | solution.py:82
  17.7 2.1 %prepare.1 = (bf16[192,192]{1,0:T(8,128)(2,1)}, bf16[192,384]{1,0:T(8,128)(2,1)}, f32[2,32,128]{2,1,0:T(8,128)}) custom-call(s32[12]{0:T(128)} %group_ref.5, bf16[27,32,12]{2,1,0:T(8,128)(2,1)} %bitcast.10, f32[1,32]{1,0:T(1,128)} %bitcast.13, bf16[27,32,32]{2,1,0:T(8,128)(2,1)} %bitcast.11, f32[1,32]{1,0:T(1,128)} %bitcast.14), custom_call_target="tpu_custom_call" | custom-call | tf_op jit(solution)/shard_map/prepare/pallas_call | solution.py:85
  19.8 15.0 %all-to-all-done = bf16[32,2,3,24,128]{4,3,2,1,0:T(8,128)(2,1)S(1)} async-done(((bf16[32,2,3,24,128]{4,3,2,1,0:T(8,128)(2,1)}), bf16[32,2,3,24,128]{4,3,2,1,0:T(8,128)(2,1)S(1)}, u32[]{:S(2)}, u32[]{:S(2)}) %all-to-all-start) | async-done | bytes 1179680 | tf_op jit(solution)/shard_map/all_to_all | solution.py:268
  34.8 0.0 copy-start
  34.8 0.0 copy-start.1
  34.8 0.0 copy-start.2
  34.8 0.0 copy-start.3
  34.8 0.1 constant_dynamic-slice_fusion.4
  34.9 4.7 %collective-permute-start.2 = (bf16[10,3,24,128]{3,2,1,0:T(8,128)(2,1)S(1)}, bf16[10,3,24,128]{3,2,1,0:T(8,128)(2,1)S(1)}, u32[]{:S(2)}, u32[]{:S(2)}) collective-permute-start(bf16[10,3,24,128]{3,2,1,0:T(8,128)(2,1)S(1)} %get-tuple-element.23), channel_id=1, source_target_pairs={{0,96},{32,64},{64,32},{96,0},{1,97},{33,65},{65,33},{97,1},{2,98}... | collective-permute-start | bytes 552968 | tf_op jit(solution)/shard_map/ppermute | solution.py:278
  39.6 0.4 collective-permute-start.1
  40.0 0.2 collective-permute-start
  40.1 0.1 constant_dynamic-slice_fusion
  40.2 2.9 %collective-permute-start.5 = (bf16[8,3,24,128]{3,2,1,0:T(8,128)(2,1)S(1)}, bf16[8,3,24,128]{3,2,1,0:T(8,128)(2,1)S(1)}, u32[]{:S(2)}, u32[]{:S(2)}) collective-permute-start(bf16[8,3,24,128]{3,2,1,0:T(8,128)(2,1)S(1)} %get-tuple-element.19), channel_id=1, source_target_pairs={{0,96},{32,64},{64,32},{96,0},{1,97},{33,65},{65,33},{97,1},{2,98}... | collective-permute-start | bytes 442376 | tf_op jit(solution)/shard_map/ppermute | solution.py:278
  43.1 0.4 collective-permute-start.4
  43.5 1.6 %collective-permute-done.2.refs_3_ = bf16[10,3,24,128]{3,2,1,0:T(8,128)(2,1)S(1)} collective-permute-done((bf16[10,3,24,128]{3,2,1,0:T(8,128)(2,1)S(1)}, bf16[10,3,24,128]{3,2,1,0:T(8,128)(2,1)S(1)}, u32[]{:S(2)}, u32[]{:S(2)}) %collective-permute-start.2) | collective-permute-done | bytes 184352 | tf_op jit(solution)/shard_map/ppermute | solution.py:278
  45.0 0.5 collective-permute-start.3
  45.5 3.5 %collective-permute-done.1.refs_2_ = bf16[10,3,24,128]{3,2,1,0:T(8,128)(2,1)S(1)} collective-permute-done((bf16[10,3,24,128]{3,2,1,0:T(8,128)(2,1)S(1)}, bf16[10,3,24,128]{3,2,1,0:T(8,128)(2,1)S(1)}, u32[]{:S(2)}, u32[]{:S(2)}) %collective-permute-start.1) | collective-permute-done | bytes 184352 | tf_op jit(solution)/shard_map/ppermute | solution.py:278
  49.0 0.0 collective-permute-done.refs_1_
  49.0 0.0 copy-done
  49.0 0.0 copy-done.1
  49.0 0.0 copy-done.2
  49.0 0.0 copy-done.3
  49.0 6.3 %head.1.refs_11_ = bf16[32,16,8,128]{3,2,1,0:T(8,128)(2,1)S(1)} custom-call(s32[12]{0:T(128)S(1)} %copy-done.3, bf16[10,3,24,128]{3,2,1,0:T(8,128)(2,1)S(1)} %get-tuple-element.26.refs_0_, bf16[10,3,24,128]{3,2,1,0:T(8,128)(2,1)S(1)} %collective-permute-done.refs_1_, bf16[10,3,24,128]{3,2,1,0:T(8,128)(2,1)S(1)} %collective-permute-done.1.refs_2_, ...), custom_call_target="tpu_custom_call" | custom-call | tf_op jit(solution)/shard_map/head/pallas_call | solution.py:236
  55.3 0.0 collective-permute-done.5.refs_7_
  55.3 0.0 collective-permute-done.4.refs_6_
  55.3 0.0 collective-permute-done.3.refs_5_
  55.3 6.9 %tail.1 = bf16[32,32,8,128]{3,2,1,0:T(8,128)(2,1)} custom-call(s32[12]{0:T(128)S(1)} %copy-done.3, bf16[10,3,24,128]{3,2,1,0:T(8,128)(2,1)S(1)} %get-tuple-element.26.refs_0_, bf16[10,3,24,128]{3,2,1,0:T(8,128)(2,1)S(1)} %collective-permute-done.refs_1_, bf16[10,3,24,128]{3,2,1,0:T(8,128)(2,1)S(1)} %collective-permute-done.1.refs_2_, ...), custom_call_target="tpu_custom_call" | custom-call | tf_op jit(solution)/shard_map/tail/pallas_call | solution.py:236
Async XLA Ops:
  6.9 9.9 %copy-start.4 = (bf16[32,12,3,3,3]{0,4,3,2,1:T(4,128)(2,1)S(1)}, bf16[32,12,3,3,3]{0,4,3,2,1:T(4,128)(2,1)}, u32[]{:S(2)}) copy-start(bf16[32,12,3,3,3]{0,4,3,2,1:T(4,128)(2,1)} %param.10) | copy-start | bytes 62212
  6.9 27.9 %all-to-all-start = ((bf16[32,2,3,24,128]{4,3,2,1,0:T(8,128)(2,1)}), bf16[32,2,3,24,128]{4,3,2,1,0:T(8,128)(2,1)S(1)}, u32[]{:S(2)}, u32[]{:S(2)}) async-start(bf16[32,2,3,24,128]{4,3,2,1,0:T(8,128)(2,1)} %cross.1), calls=%async_computation | async-start | bytes 2359296 | tf_op jit(solution)/shard_map/all_to_all | solution.py:268
  34.8 14.2 %copy-start = (bf16[192,384]{1,0:T(8,128)(2,1)S(1)}, bf16[192,384]{1,0:T(8,128)(2,1)}, u32[]{:S(2)}) copy-start(bf16[192,384]{1,0:T(8,128)(2,1)} %get-tuple-element.17.refs_5_.refs_9_) | copy-start | bytes 442372
  34.8 14.2 %copy-start.1 = (bf16[192,192]{1,0:T(8,128)(2,1)S(1)}, bf16[192,192]{1,0:T(8,128)(2,1)}, u32[]{:S(2)}) copy-start(bf16[192,192]{1,0:T(8,128)(2,1)} %get-tuple-element.16.refs_4_.refs_8_) | copy-start | bytes 221188
  34.8 14.2 %copy-start.2 = (f32[2,32,128]{2,1,0:T(8,128)S(1)}, f32[2,32,128]{2,1,0:T(8,128)}, u32[]{:S(2)}) copy-start(f32[2,32,128]{2,1,0:T(8,128)} %get-tuple-element.18.refs_6_.refs_10_) | copy-start | bytes 98308
  34.8 14.2 %copy-start.3 = (s32[12]{0:T(128)S(1)}, s32[12]{0:T(128)}, u32[]{:S(2)}) copy-start(s32[12]{0:T(128)} %group_ref.5) | copy-start | bytes 148
  34.9 10.1 %collective-permute-start.2 = (bf16[10,3,24,128]{3,2,1,0:T(8,128)(2,1)S(1)}, bf16[10,3,24,128]{3,2,1,0:T(8,128)(2,1)S(1)}, u32[]{:S(2)}, u32[]{:S(2)}) collective-permute-start(bf16[10,3,24,128]{3,2,1,0:T(8,128)(2,1)S(1)} %get-tuple-element.23), channel_id=1, source_target_pairs={{0,96},{32,64},{64,32},{96,0},{1,97},{33,65},{65,33},{97,1},{2,98}... | collective-permute-start | bytes 552968 | tf_op jit(solution)/shard_map/ppermute | solution.py:278
  39.6 9.4 %collective-permute-start.1 = (bf16[10,3,24,128]{3,2,1,0:T(8,128)(2,1)S(1)}, bf16[10,3,24,128]{3,2,1,0:T(8,128)(2,1)S(1)}, u32[]{:S(2)}, u32[]{:S(2)}) collective-permute-start(bf16[10,3,24,128]{3,2,1,0:T(8,128)(2,1)S(1)} %get-tuple-element.24), channel_id=1, source_target_pairs={{0,64},{32,96},{64,0},{96,32},{1,65},{33,97},{65,1},{97,33},{2,66}... | collective-permute-start | bytes 552968 | tf_op jit(solution)/shard_map/ppermute | solution.py:278
  40.0 9.0 %collective-permute-start = (bf16[10,3,24,128]{3,2,1,0:T(8,128)(2,1)S(1)}, bf16[10,3,24,128]{3,2,1,0:T(8,128)(2,1)S(1)}, u32[]{:S(2)}, u32[]{:S(2)}) collective-permute-start(bf16[10,3,24,128]{3,2,1,0:T(8,128)(2,1)S(1)} %get-tuple-element.25), channel_id=1, source_target_pairs={{0,32},{32,0},{64,96},{96,64},{1,33},{33,1},{65,97},{97,65},{2,34}... | collective-permute-start | bytes 552968 | tf_op jit(solution)/shard_map/ppermute | solution.py:278
  40.2 15.1 %collective-permute-start.5 = (bf16[8,3,24,128]{3,2,1,0:T(8,128)(2,1)S(1)}, bf16[8,3,24,128]{3,2,1,0:T(8,128)(2,1)S(1)}, u32[]{:S(2)}, u32[]{:S(2)}) collective-permute-start(bf16[8,3,24,128]{3,2,1,0:T(8,128)(2,1)S(1)} %get-tuple-element.19), channel_id=1, source_target_pairs={{0,96},{32,64},{64,32},{96,0},{1,97},{33,65},{65,33},{97,1},{2,98}... | collective-permute-start | bytes 442376 | tf_op jit(solution)/shard_map/ppermute | solution.py:278
  43.1 12.2 %collective-permute-start.4 = (bf16[8,3,24,128]{3,2,1,0:T(8,128)(2,1)S(1)}, bf16[8,3,24,128]{3,2,1,0:T(8,128)(2,1)S(1)}, u32[]{:S(2)}, u32[]{:S(2)}) collective-permute-start(bf16[8,3,24,128]{3,2,1,0:T(8,128)(2,1)S(1)} %get-tuple-element.20), channel_id=1, source_target_pairs={{0,64},{32,96},{64,0},{96,32},{1,65},{33,97},{65,1},{97,33},{2,66}... | collective-permute-start | bytes 442376 | tf_op jit(solution)/shard_map/ppermute | solution.py:278
  45.0 10.3 %collective-permute-start.3 = (bf16[8,3,24,128]{3,2,1,0:T(8,128)(2,1)S(1)}, bf16[8,3,24,128]{3,2,1,0:T(8,128)(2,1)S(1)}, u32[]{:S(2)}, u32[]{:S(2)}) collective-permute-start(bf16[8,3,24,128]{3,2,1,0:T(8,128)(2,1)S(1)} %get-tuple-element.21), channel_id=1, source_target_pairs={{0,32},{32,0},{64,96},{96,64},{1,33},{33,1},{65,97},{97,65},{2,34}... | collective-permute-start | bytes 442376 | tf_op jit(solution)/shard_map/ppermute | solution.py:278
